TPU v7x, 256 devices: a whole 4x4x8 slice. The times are simulated.
256 devices in a mesh: section: 2 (over core), req: 128 (over x, y, z).
Axes of the slice: x: 4, y: 4, z: 8, core: 2. Of those that a mesh axis runs over, the one named last changes fastest.
Arguments:
- section_in: bfloat16 [2, 128, 32, 1152], P('section', 'req'), may hold values from -24 to 24
- patch_index: int32 [2, 128], P('section', 'req'), may hold values from 0 to 3
- stale_kv: bfloat16 [2, 128, 128, 2304], P('section', 'req'), may hold values from -400 to 400
- modulation: float32 [2, 128, 6, 1152], P('section', 'req'), may hold values from -4 to 4
- final_mod: float32 [128, 2, 1152], P('req'), may hold values from -4 to 4
- qkv_blocks: bfloat16 [2, 128, 1152, 864], P('section', 'req'), may hold values from -1 to 1, as said below
- out_blocks: bfloat16 [2, 128, 1152, 288], P('section', 'req'), may hold values from -1 to 1, as said below
- up_blocks: bfloat16 [2, 128, 1152, 1152], P('section', 'req'), may hold values from -1 to 1, as said below
- down_blocks: bfloat16 [2, 128, 1152, 1152], P('section', 'req'), may hold values from -1 to 1, as said below
- final_weight: bfloat16 [1152, 16], replicated, may hold values from -0.1875 to 0.1875
- noisy_latent: float32 [128, 512], P('req', 'section'), may hold values from -6 to 6
- time_index: int32 [128], P('req'), may hold values from 100 to 499
- time_gap: int32 [128], P('req'), may hold values from 10 to 40
Outputs:
- fresh_kv: bfloat16 [2, 128, 32, 2304], P('section', 'req')
- next_input: bfloat16 [128, 32, 1152], P('req', 'section')
- noise_pred: float32 [128, 512], P('req', 'section')
- denoised: float32 [128, 512], P('req', 'section')
Inputs may be any that keep to these rules, and one draw needn't show every extreme that they name: qkv_blocks[s, r] equals qkv_blocks[s, r mod 4]. out_blocks[s, r] equals out_blocks[s, r mod 4]. up_blocks[s, r] equals up_blocks[s, r mod 4]. down_blocks[s, r] equals down_blocks[s, r mod 4].
All inputs are finite; a program needn't handle non-finite values.
Results may differ from a plain program's by a relative error of at most 0.0093.
Values may be sent and summed in bfloat16 or wider, within the bound.
A program may use at most 64 MiB of HBM per device.

v0:
```python
from functools import partial

import jax
import jax.numpy as jnp
from jax import lax
from jax.sharding import PartitionSpec as P

HEADS = 16
UNIT_GROUPS = 4


NORM_EPS = 1e-06
BETA_LOW = 0.0001
BETA_HIGH = 0.02


def from_partner(x, axis, bit):
    return lax.ppermute(x, axis, [(i, i ^ 1 << bit) for i in range(lax.axis_size(axis))])


def layer_norm(values):
    average = jnp.mean(values, axis=-1, keepdims=True)
    centred = values - average
    spread = jnp.mean(centred * centred, axis=-1, keepdims=True)
    return centred * lax.rsqrt(spread + NORM_EPS)


def alpha_bar(step_index):
    moment = step_index.astype(jnp.float32)
    return jnp.exp(
        -(BETA_LOW * (moment + 1.0) + (BETA_HIGH - BETA_LOW) * moment * (moment + 1.0) / 1998.0)
    )


def attend(queries, fresh_keys, fresh_values, stale_rows, patch_at):
    fresh_count = queries.shape[0]
    model_width = queries.shape[1]
    head_size = model_width // HEADS
    fresh_rows = jnp.concatenate([fresh_keys, fresh_values], axis=1)
    start = patch_at * fresh_count
    all_rows = lax.dynamic_update_slice(stale_rows, fresh_rows, (start, jnp.zeros((), jnp.int32)))
    key_rows = all_rows[:, :model_width]
    value_rows = all_rows[:, model_width:]
    scores = jnp.einsum(
        "qhd,khd->hqk",
        queries.reshape(fresh_count, HEADS, head_size),
        key_rows.reshape(-1, HEADS, head_size),
        preferred_element_type=jnp.float32,
    ) * head_size ** (-0.5)
    highest = jnp.max(scores, axis=-1, keepdims=True)
    raised = jnp.exp(scores - highest)
    attention_weights = (raised / jnp.sum(raised, axis=-1, keepdims=True)).astype(jnp.bfloat16)
    mixed = jnp.einsum(
        "hqk,khd->qhd",
        attention_weights,
        value_rows.reshape(-1, HEADS, head_size),
        preferred_element_type=jnp.float32,
    )
    return mixed.reshape(fresh_count, model_width).astype(jnp.bfloat16)


def block_product(incoming, weight):
    return jnp.einsum("nsd,dc->nsc", incoming, weight, preferred_element_type=jnp.float32).astype(
        jnp.bfloat16
    )


def unit_block(incoming, w_up, w_down):
    inner = jax.nn.gelu(
        jnp.einsum("nsd,df->nsf", incoming, w_up, preferred_element_type=jnp.float32),
        approximate=True,
    ).astype(jnp.bfloat16)
    return jnp.einsum("nsf,fd->nsd", inner, w_down, preferred_element_type=jnp.float32).astype(
        jnp.bfloat16
    )


def spread_regroup(token_rows, block_fn, staggered):
    devices = lax.axis_size("req")
    slices = devices // UNIT_GROUPS
    feature = token_rows.shape[1]
    per_slice = token_rows.shape[0] // slices
    pieces = token_rows.reshape(slices, per_slice, feature)
    outgoing = jnp.broadcast_to(pieces[:, None], (slices, UNIT_GROUPS, per_slice, feature)).reshape(
        devices, per_slice, feature
    )
    returned = lax.all_to_all(
        block_fn(lax.all_to_all(outgoing, "req", split_axis=0, concat_axis=0, tiled=True)),
        "req",
        split_axis=0,
        concat_axis=0,
        tiled=True,
    )
    columns = returned.shape[-1]
    ordered = returned.reshape(slices, UNIT_GROUPS, per_slice, columns).transpose(0, 2, 1, 3)
    return ordered.reshape(slices * per_slice, UNIT_GROUPS, columns)


def layer_step(hidden, stale_rows, mods, patch_at, w_qkv, w_out, w_up, w_down, regroup):
    fresh_count = hidden.shape[0]
    model_width = hidden.shape[1]
    residual = hidden.astype(jnp.float32)
    normed = (layer_norm(residual) * (1.0 + mods[1]) + mods[0]).astype(jnp.bfloat16)
    joined = regroup(normed, partial(block_product, weight=w_qkv))
    joined = joined.reshape(fresh_count, UNIT_GROUPS, 3, model_width // UNIT_GROUPS)
    queries = joined[:, :, 0].reshape(fresh_count, model_width)
    fresh_keys = joined[:, :, 1].reshape(fresh_count, model_width)
    fresh_values = joined[:, :, 2].reshape(fresh_count, model_width)
    mixed = attend(queries, fresh_keys, fresh_values, stale_rows, patch_at)
    projected = regroup(mixed, partial(block_product, weight=w_out)).reshape(
        fresh_count, model_width
    )
    after_attention = residual + mods[2] * projected.astype(jnp.float32)
    middle = (layer_norm(after_attention) * (1.0 + mods[4]) + mods[3]).astype(jnp.bfloat16)
    parts = regroup(middle, partial(unit_block, w_up=w_up, w_down=w_down))
    total = jnp.sum(parts.astype(jnp.float32), axis=1)
    layer_out = (after_attention + mods[5] * total).astype(jnp.bfloat16)
    return (layer_out, jnp.concatenate([fresh_keys, fresh_values], axis=1))


def per_device(
    section_in,
    patch_index,
    stale_kv,
    modulation,
    final_mod,
    qkv_blocks,
    out_blocks,
    up_blocks,
    down_blocks,
    final_weight,
    noisy_latent,
    time_index,
    time_gap,
):
    regroup = partial(spread_regroup, staggered=False)
    hidden = section_in[0, 0]
    layer_out, fresh = layer_step(
        hidden,
        stale_kv[0, 0],
        modulation[0, 0],
        patch_index[0, 0],
        qkv_blocks[0, 0],
        out_blocks[0, 0],
        up_blocks[0, 0],
        down_blocks[0, 0],
        regroup,
    )
    half_rows = hidden.shape[0] // 2
    upper = layer_out[:half_rows]
    lower = layer_out[half_rows:]
    section_id = lax.axis_index("section")
    leaving = jnp.where(section_id == 0, lower, upper)
    arrived = from_partner(leaving, "section", 0)
    next_rows = jnp.where(section_id == 0, upper, arrived)
    final_rows = jnp.where(section_id == 0, arrived, lower)
    shifted = (
        layer_norm(final_rows.astype(jnp.float32)) * (1.0 + final_mod[0, 1]) + final_mod[0, 0]
    ).astype(jnp.bfloat16)
    noise_pred = jnp.dot(shifted, final_weight, preferred_element_type=jnp.float32).reshape(1, -1)
    now_bar = alpha_bar(time_index[0])
    prev_bar = alpha_bar(time_index[0] - time_gap[0])
    clean_latent = (noisy_latent - jnp.sqrt(1.0 - now_bar) * noise_pred) / jnp.sqrt(now_bar)
    denoised = jnp.sqrt(prev_bar) * clean_latent + jnp.sqrt(1.0 - prev_bar) * noise_pred
    return (fresh[None, None], next_rows[None], noise_pred, denoised)


def solution(mesh):
    placed = (
        P("section", "req", None, None),
        P("section", "req"),
        P("section", "req", None, None),
        P("section", "req", None, None),
        P("req", None, None),
        P("section", "req", None, None),
        P("section", "req", None, None),
        P("section", "req", None, None),
        P("section", "req", None, None),
        P(),
        P("req", "section"),
        P("req"),
        P("req"),
    )
    return jax.shard_map(
        per_device,
        mesh=mesh,
        in_specs=placed,
        out_specs=(
            P("section", "req", None, None),
            P("req", "section", None),
            P("req", "section"),
            P("req", "section"),
        ),
        check_vma=False,
    )
```

profile of v0, /device:TPU:1, one launch (start us, length us, event | category | flops | bytes accessed | tf_op | source)
XLA Modules:
  0.0 197.4 jit_solution(18322283972901654462)
XLA Ops:
  0.6 2.1 %copy.78 = bf16[1,1,128,2304]{3,2,1,0:T(8,128)(2,1)} copy(bf16[1,1,128,2304]{3,2,1,0:T(8,128)(2,1)} %param.15) | data formatting | bytes 1179648
  2.7 1.4 slice_reduce_fusion.5
  4.1 1.0 convert_reduce_fusion.2
  5.2 1.1 fusion.54
  6.2 1.0 fusion.57
  7.3 0.2 broadcast_in_dim.46
  7.5 0.5 broadcast.213
  8.0 2.4 %reduce.28 = bf16[128,1152]{1,0:T(8,128)(2,1)S(1)} reduce(bf16[128,1,1152]{2,1,0:T(2,128)(2,1)S(1)} %broadcast_in_dim.46, bf16[]{:T(256)} %broadcast.213), dimensions={1}, to_apply=%broadcast_in_dim.46.reduce_sub_computation | reduce | bytes 589826 | tf_op jit(solution)/shard_map/broadcast_in_dim | solution.py:84
  10.4 0.3 reshape.360
  10.8 31.4 %all_to_all.30 = bf16[128,2,576]{2,1,0:T(2,128)(2,1)} all-to-all(bf16[128,2,576]{2,1,0:T(2,128)(2,1)S(1)} %reshape.360), channel_id=1, replica_groups=mesh['section'=2,'req'=128] {'req'}, dimensions={0} | all-to-all | bytes 589824 | tf_op jit(solution)/shard_map/all_to_all | solution.py:88
  42.1 2.5 %reshape.361 = bf16[128,1,1152]{2,1,0:T(2,128)(2,1)S(1)} reshape(bf16[128,2,576]{2,1,0:T(2,128)(2,1)} %all_to_all.30) | data formatting | bytes 589824
  44.7 2.2 %fusion.18 = bf16[128,1,864]{0,2,1:T(8,128)(2,1)S(1)} fusion(bf16[1,1,1152,864]{2,3,1,0:T(8,128)(2,1)} %param.18, bf16[128,1,1152]{2,1,0:T(2,128)(2,1)S(1)} %reshape.361), kind=kOutput, calls=%fused_computation.13 | convolution fusion | flops 254914560 | bytes 2506752 | tf_op jit(solution)/shard_map/nsd,dc->nsc/dot_general | solution.py:63
  46.9 0.8 reduce.29
  47.7 0.2 copy.69
  47.9 1.0 reshape.362
  48.8 6.6 %all-to-all-start.1 = ((bf16[128,2,432]{2,1,0:T(2,128)(2,1)}), bf16[128,2,432]{2,1,0:T(2,128)(2,1)S(1)}, u32[]{:S(2)}, u32[]{:S(2)}) async-start(bf16[128,2,432]{2,1,0:T(2,128)(2,1)} %reshape.362), calls=%async_computation.1 | async-start | bytes 524288 | tf_op jit(solution)/shard_map/all_to_all | solution.py:87
  56.1 11.9 %all-to-all-done.1 = bf16[128,2,432]{2,1,0:T(2,128)(2,1)S(1)} async-done(((bf16[128,2,432]{2,1,0:T(2,128)(2,1)}), bf16[128,2,432]{2,1,0:T(2,128)(2,1)S(1)}, u32[]{:S(2)}, u32[]{:S(2)}) %all-to-all-start.1) | async-done | bytes 221216 | tf_op jit(solution)/shard_map/all_to_all | solution.py:87
  67.9 0.5 reshape.363
  68.4 1.4 reduce.3
  69.9 0.3 reshape_reshape_transpose_reshape.4
  70.1 2.2 %slice_reduce_fusion = (bf16[32,4,288]{2,1,0:T(4,128)(2,1)}, bf16[32,4,288]{2,1,0:T(4,128)(2,1)S(1)}, bf16[32,4,288]{2,1,0:T(4,128)(2,1)S(1)}) fusion(bf16[32,4,3,288]{3,2,1,0:T(4,128)(2,1)S(1)} %reshape_reshape_transpose_reshape.4), kind=kLoop, calls=%fused_computation.40 | loop fusion | bytes 442368 | tf_op jit(solution)/shard_map/slice | solution.py:106
  72.7 0.7 copy-done.2
  73.3 0.7 constant_dynamic-update-slice_fusion.2
  74.0 1.1 fusion.78
  75.1 0.2 copy.43
  75.3 1.7 reshape_reshape_squeeze.3
  77.0 1.1 convolution_multiply_fusion
  78.1 0.2 fusion.79
  78.3 0.2 copy.42
  78.5 0.9 fusion.21
  79.5 0.2 convert_element_type.110
  79.8 0.2 broadcast_in_dim.47
  80.0 2.4 %reduce.30 = bf16[128,1152]{1,0:T(8,128)(2,1)S(1)} reduce(bf16[128,1,1152]{2,1,0:T(2,128)(2,1)S(1)} %broadcast_in_dim.47, bf16[]{:T(256)} %broadcast.213), dimensions={1}, to_apply=%broadcast_in_dim.47.reduce_sub_computation | reduce | bytes 589826 | tf_op jit(solution)/shard_map/broadcast_in_dim | solution.py:84
  82.4 0.3 reshape.364
  82.8 19.7 %all_to_all.31 = bf16[128,2,576]{2,1,0:T(2,128)(2,1)} all-to-all(bf16[128,2,576]{2,1,0:T(2,128)(2,1)S(1)} %reshape.364), channel_id=1, replica_groups=mesh['section'=2,'req'=128] {'req'}, dimensions={0} | all-to-all | bytes 589824 | tf_op jit(solution)/shard_map/all_to_all | solution.py:88
  102.4 2.5 %reshape.365 = bf16[128,1,1152]{2,1,0:T(2,128)(2,1)S(1)} reshape(bf16[128,2,576]{2,1,0:T(2,128)(2,1)} %all_to_all.31) | data formatting | bytes 589824
  105.0 1.4 fusion.22
  106.4 0.7 reduce.31
  107.3 16.9 %all_to_all.32 = bf16[128,2,144]{2,1,0:T(2,128)(2,1)S(1)} all-to-all(bf16[128,2,144]{2,1,0:T(2,128)(2,1)S(1)} %reshape.366), channel_id=1, replica_groups=mesh['section'=2,'req'=128] {'req'}, dimensions={0} | all-to-all | bytes 147456 | tf_op jit(solution)/shard_map/all_to_all | solution.py:87
  124.2 0.2 reshape.367
  124.3 0.5 convert_reduce_fusion.1
  125.0 0.1 fusion.77
  125.2 0.2 multiply_reduce_fusion
  125.5 0.8 broadcast_in_dim.21
  126.3 2.1 %broadcast_in_dim.48 = bf16[128,1,1152]{2,1,0:T(2,128)(2,1)S(1)} reshape(bf16[32,4,1152]{2,1,0:T(4,128)(2,1)} %broadcast_in_dim.21) | data formatting | bytes 589824 | tf_op jit(solution)/shard_map/broadcast_in_dim | solution.py:84
  128.4 3.2 %reduce.32 = bf16[128,1152]{1,0:T(8,128)(2,1)} reduce(bf16[128,1,1152]{2,1,0:T(2,128)(2,1)S(1)} %broadcast_in_dim.48, bf16[]{:T(256)} %broadcast.213), dimensions={1}, to_apply=%broadcast_in_dim.48.reduce_sub_computation | reduce | bytes 589826 | tf_op jit(solution)/shard_map/broadcast_in_dim | solution.py:84
  131.6 1.3 reshape.368
  132.9 18.8 %all_to_all.33 = bf16[128,2,576]{2,1,0:T(2,128)(2,1)S(1)} all-to-all(bf16[128,2,576]{2,1,0:T(2,128)(2,1)S(1)} %reshape.368), channel_id=1, replica_groups=mesh['section'=2,'req'=128] {'req'}, dimensions={0} | all-to-all | bytes 589824 | tf_op jit(solution)/shard_map/all_to_all | solution.py:88
  151.6 1.2 reshape.369
  152.8 3.0 %fusion.8 = bf16[128,1,1152]{2,0,1:T(8,128)(2,1)S(1)} fusion(bf16[1,1,1152,1152]{3,2,1,0:T(8,128)(2,1)S(1)} %copy-done, bf16[1,1,1152,1152]{3,2,1,0:T(8,128)(2,1)} %param.20, bf16[128,1,1152]{2,1,0:T(2,128)(2,1)} %reshape.369), kind=kOutput, calls=%fused_computation.6 | convolution fusion | flops 680951808 | bytes 5898240 | tf_op jit(solution)/shard_map/nsf,fd->nsd/dot_general | solution.py:73
  155.9 0.8 reduce.33
  156.7 1.1 reshape.370
  157.7 7.6 %all-to-all-start.5 = ((bf16[128,2,576]{2,1,0:T(2,128)(2,1)}), bf16[128,2,576]{2,1,0:T(2,128)(2,1)}, u32[]{:S(2)}, u32[]{:S(2)}) async-start(bf16[128,2,576]{2,1,0:T(2,128)(2,1)} %reshape.370), calls=%async_computation.5 | async-start | bytes 655360 | tf_op jit(solution)/shard_map/all_to_all | solution.py:87
  165.4 12.6 %all-to-all-done.5 = bf16[128,2,576]{2,1,0:T(2,128)(2,1)} async-done(((bf16[128,2,576]{2,1,0:T(2,128)(2,1)}), bf16[128,2,576]{2,1,0:T(2,128)(2,1)}, u32[]{:S(2)}, u32[]{:S(2)}) %all-to-all-start.5) | async-done | bytes 294944 | tf_op jit(solution)/shard_map/all_to_all | solution.py:87
  178.0 2.5 %reshape.371 = bf16[128,1,1152]{2,1,0:T(2,128)(2,1)S(1)} reshape(bf16[128,2,576]{2,1,0:T(2,128)(2,1)} %all-to-all-done.5) | data formatting | bytes 589824
  180.5 2.4 %convert_reduce_fusion = f32[128,1152]{1,0:T(8,128)} fusion(bf16[128,1,1152]{2,1,0:T(2,128)(2,1)S(1)} %reshape.371), kind=kLoop, calls=%fused_computation.28 | loop fusion | flops 147456 | bytes 884736 | tf_op jit(solution)/shard_map/convert_element_type | solution.py:116
  182.9 1.2 reshape.329
  184.2 1.0 reduce_sum.77
  185.2 0.9 add_convert_fusion
  186.1 7.8 %collective-permute-start = (bf16[16,1152]{1,0:T(8,128)(2,1)S(1)}, bf16[16,1152]{1,0:T(8,128)(2,1)S(1)}, u32[]{:S(2)}, u32[]{:S(2)}) collective-permute-start(bf16[16,1152]{1,0:T(8,128)(2,1)S(1)} %broadcast_select_fusion.1), channel_id=1, source_target_pairs={{0,128},{128,0},{1,129},{129,1},{2,130},{130,2},{3,131},{131,3},{4... | collective-permute-start | bytes 110600 | tf_op jit(solution)/shard_map/ppermute | solution.py:18
  195.7 0.2 fusion.62
  195.9 0.2 fusion.66
  196.2 0.6 multiply_add_fusion
  196.8 0.6 select_bitcast_fusion
  (39 shorter events, 1.3 us)
Async XLA Ops:
  0.6 152.2 %copy-start = (bf16[1,1,1152,1152]{3,2,1,0:T(8,128)(2,1)S(1)}, bf16[1,1,1152,1152]{3,2,1,0:T(8,128)(2,1)}, u32[]{:S(2)}) copy-start(bf16[1,1,1152,1152]{3,2,1,0:T(8,128)(2,1)} %param.21) | copy-start | bytes 7962628
  48.8 19.1 %all-to-all-start.1 = ((bf16[128,2,432]{2,1,0:T(2,128)(2,1)}), bf16[128,2,432]{2,1,0:T(2,128)(2,1)S(1)}, u32[]{:S(2)}, u32[]{:S(2)}) async-start(bf16[128,2,432]{2,1,0:T(2,128)(2,1)} %reshape.362), calls=%async_computation.1 | async-start | bytes 524288 | tf_op jit(solution)/shard_map/all_to_all | solution.py:87
  72.6 0.7 copy-start.2
  82.4 42.6 %copy-start.1 = (bf16[1,1,32,1152]{3,2,1,0:T(8,128)(2,1)S(1)}, bf16[1,1,32,1152]{3,2,1,0:T(8,128)(2,1)}, u32[]{:S(2)}) copy-start(bf16[1,1,32,1152]{3,2,1,0:T(8,128)(2,1)} %param.13) | copy-start | bytes 221188
  82.7 42.6 %copy-start.3 = (f32[1152]{0:T(1024)S(1)}, f32[1152]{0:T(1024)}, u32[]{:S(2)}) copy-start(f32[1152]{0:T(1024)} %get-tuple-element.11) | copy-start | bytes 13828
  82.7 42.6 %copy-start.4 = (f32[1152]{0:T(1024)S(1)}, f32[1152]{0:T(1024)}, u32[]{:S(2)}) copy-start(f32[1152]{0:T(1024)} %get-tuple-element.12) | copy-start | bytes 13828
  157.7 36.2 %copy-start.5 = (f32[1,2,1152]{2,1,0:T(2,128)S(1)}, f32[1,2,1152]{2,1,0:T(2,128)}, u32[]{:S(2)}) copy-start(f32[1,2,1152]{2,1,0:T(2,128)} %param.17) | copy-start | bytes 27652
  157.7 38.2 %copy-start.8 = (bf16[1152,16]{0,1:T(8,128)(2,1)S(1)}, bf16[1152,16]{0,1:T(8,128)(2,1)}, u32[]{:S(2)}) copy-start(bf16[1152,16]{0,1:T(8,128)(2,1)} %param.22) | copy-start | bytes 110596
  157.7 20.2 %all-to-all-start.5 = ((bf16[128,2,576]{2,1,0:T(2,128)(2,1)}), bf16[128,2,576]{2,1,0:T(2,128)(2,1)}, u32[]{:S(2)}, u32[]{:S(2)}) async-start(bf16[128,2,576]{2,1,0:T(2,128)(2,1)} %reshape.370), calls=%async_computation.5 | async-start | bytes 655360 | tf_op jit(solution)/shard_map/all_to_all | solution.py:87
  165.4 30.9 %copy-start.7 = (f32[1,256]{1,0:T(1,128)S(1)}, f32[1,256]{1,0:T(1,128)}, u32[]{:S(2)}) copy-start(f32[1,256]{1,0:T(1,128)} %param.23) | copy-start | bytes 3076
  186.1 9.4 %collective-permute-start = (bf16[16,1152]{1,0:T(8,128)(2,1)S(1)}, bf16[16,1152]{1,0:T(8,128)(2,1)S(1)}, u32[]{:S(2)}, u32[]{:S(2)}) collective-permute-start(bf16[16,1152]{1,0:T(8,128)(2,1)S(1)} %broadcast_select_fusion.1), channel_id=1, source_target_pairs={{0,128},{128,0},{1,129},{129,1},{2,130},{130,2},{3,131},{131,3},{4... | collective-permute-start | bytes 110600 | tf_op jit(solution)/shard_map/ppermute | solution.py:18
  196.2 1.2 copy-start.6
where the time goes:
time: 199 us; the launch traced here: 197 us
  blocking collectives  86.7 us (44%)
  local copies, waits for them, and re-layouts  28.8 us (14%)
  waiting for transfers between devices  24.5 us (12%)
  other arithmetic  23.4 us (12%)
  starting transfers between devices  22 us (11%)
  matrix products  8.92 us (4%)
  between operations  3.2 us (2%)
    all_to_all x3, blocking collectives, spread_regroup(): lax.all_to_all(outgoing, 'req', split_axis=0, concat_axis=0, tiled=True)  69.8 us
    all_to_all x2, waiting for transfers between devices, spread_regroup(): lax.all_to_all(block_fn(lax.all_to_all(outgoing, 'req', split_axis=0, con...  24.5 us
    all_to_all x1, blocking collectives, spread_regroup(): lax.all_to_all(block_fn(lax.all_to_all(outgoing, 'req', split_axis=0, con...  16.9 us
    unnamed x34, local copies, waits for them, and re-layouts  16.5 us
    all_to_all x2, starting transfers between devices, spread_regroup(): lax.all_to_all(block_fn(lax.all_to_all(outgoing, 'req', split_axis=0, con...  14.2 us
    broadcast_in_dim x3, other arithmetic, spread_regroup(): jnp.broadcast_to(pieces[:, None], (slices, UNIT_GROUPS, per_slice, feature))  7.97 us
    ppermute x1, starting transfers between devices, from_partner(): lax.ppermute(x, axis, [(i, i ^ 1 << bit) for i in range(lax.axis_size(axi...  7.83 us
  transfers between devices with their start and end apart: 3, of which 2 were waited for; matrix products, arithmetic and copies ran while one was open for 0% of the time, Pallas kernels for 0%

commit v1 on v0

v1 whole, which is shorter than its diff:
```python
import functools

import jax
import jax.numpy as jnp
from jax import lax
from jax.experimental import pallas as pl
from jax.experimental.pallas import tpu as pltpu
from jax.sharding import PartitionSpec as P

MESH = pl.DeviceIdType.MESH
HEADS = 16
GROUPS = 4
NORM_EPS = 1e-06
BETA_LOW = 0.0001
BETA_HIGH = 0.02
TOK = 32
D = 1152
BW = D // GROUPS
HEAD = D // HEADS
KEEP = 96
KVW = 640
WIN = 384
RING = 8
F32 = jnp.float32
BF16 = jnp.bfloat16


def layer_norm(values):
    average = jnp.mean(values, axis=-1, keepdims=True)
    centred = values - average
    spread = jnp.mean(centred * centred, axis=-1, keepdims=True)
    return centred * lax.rsqrt(spread + NORM_EPS)


def alpha_bar(moment):
    return jnp.exp(
        -(BETA_LOW * (moment + 1.0) + (BETA_HIGH - BETA_LOW) * moment * (moment + 1.0) / 1998.0)
    )


def kernel(
    patch_ref,
    time_ref,
    gap_ref,
    h_hbm,
    stale_hbm,
    mod_hbm,
    fmod_hbm,
    wq_hbm,
    wo_hbm,
    wu_hbm,
    wd_hbm,
    fw_hbm,
    noisy_hbm,
    fresh_out,
    next_out,
    noise_out,
    den_out,
    h_v,
    st_v,
    mod_v,
    fmod_v,
    wq_v,
    wo_v,
    wu_v,
    wd_v,
    fw_v,
    noisy_v,
    x1,
    x2,
    kvs,
    kvb,
    fk,
    attn_v,
    inner_v,
    ps,
    r2,
    parts,
    r4,
    leave,
    arrive,
    lsem,
    ssem,
    rsem,
):
    s = lax.axis_index("section")
    r = lax.axis_index("req")
    z = lax.rem(r, RING)
    base = r - z
    odd = lax.rem(z, 2)
    mine = lax.rem(z, GROUPS)

    def at(dz):
        return (s, base + lax.rem(z + dz + RING, RING))

    far = 2 - 4 * odd
    outward = [
        (at(1), lax.rem(z + 1, GROUPS), 2),
        (at(-1), lax.rem(z + 3, GROUPS), 1),
        (at(far), lax.rem(z + 2, GROUPS), 3),
    ]
    homeward = [(1, at(1), 2), (2, at(-1), 1), (3, at(-far), 3)]
    other = (1 - s, r)

    local = []

    def load(i, src, dst):
        copy = pltpu.make_async_copy(src, dst, lsem.at[i])
        copy.start()
        local.append(copy)
        return copy

    c_h = load(0, h_hbm, h_v)
    c_mod = load(1, mod_hbm, mod_v)
    c_st = load(2, stale_hbm, st_v)
    c_wq = load(3, wq_hbm, wq_v)

    barrier = pltpu.get_barrier_semaphore()
    for peer in (at(1), at(-1), at(2), at(-2), other):
        pl.semaphore_signal(barrier, inc=1, device_id=peer, device_id_type=MESH)

    wo_v[:, 0:TOK, :] = jnp.zeros((GROUPS, TOK, BW), BF16)
    wo_v[:, TOK + BW :, :] = jnp.zeros((GROUPS, WIN - TOK - BW, BW), BF16)
    c_wo = load(4, wo_hbm.at[pl.ds(mine * BW, BW), :], wo_v.at[mine, pl.ds(TOK, BW), :])
    c_wu = load(5, wu_hbm, wu_v)
    c_wd = load(6, wd_hbm, wd_v)
    c_fw = load(7, fw_hbm, fw_v)
    c_fm = load(8, fmod_hbm, fmod_v)
    c_nz = load(9, noisy_hbm, noisy_v)

    sends = []
    count = [0]

    def remote(src, dst, device):
        i = count[0]
        count[0] += 1
        copy = pltpu.make_async_remote_copy(
            src_ref=src,
            dst_ref=dst,
            send_sem=ssem.at[i],
            recv_sem=rsem.at[i],
            device_id=device,
            device_id_type=MESH,
        )
        copy.start()
        sends.append(copy)
        return copy

    c_h.wait()
    c_mod.wait()
    normed = layer_norm(h_v[...].astype(F32)) * (1.0 + mod_v[1:2, :]) + mod_v[0:1, :]
    x1[0] = normed.astype(BF16)

    c_st.wait()
    patch = patch_ref[0, 0]
    for k in range(3):
        low = st_v[k * TOK : (k + 1) * TOK, :].astype(F32)
        high = st_v[(k + 1) * TOK : (k + 2) * TOK, :].astype(F32)
        kept = jnp.where(patch <= k, high, low)
        for j in range(GROUPS):
            kvs[j, k * TOK : (k + 1) * TOK, :] = jnp.concatenate(
                [
                    kept[:, j * BW : (j + 1) * BW],
                    kept[:, D + j * BW : D + (j + 1) * BW],
                    jnp.zeros((TOK, KVW - 2 * BW), F32),
                ],
                axis=1,
            ).astype(BF16)
    kvb[0, 0:KEEP, :] = kvs[mine]

    pl.semaphore_wait(barrier, 5)
    c_x = [remote(x1.at[0], x1.at[slot], dev) for dev, _, slot in outward]
    c_kv = [
        remote(kvs.at[res], kvb.at[slot, pl.ds(0, KEEP), :], dev) for dev, res, slot in outward
    ]
    c_w = [
        remote(
            wo_hbm.at[pl.ds(res * BW, BW), :],
            wo_v.at[mine, pl.ds(TOK, BW), :],
            dev,
        )
        for dev, res, _ in outward
    ]

    c_wq.wait()
    for c in c_x:
        c.wait_recv()
    qkv = jnp.dot(x1[...].reshape(GROUPS * TOK, D), wq_v[...], preferred_element_type=F32)
    fresh = jnp.concatenate(
        [qkv[:, BW:], jnp.zeros((GROUPS * TOK, KVW - 2 * BW), F32)], axis=1
    ).astype(BF16)
    for slot in range(GROUPS):
        kvb[slot, KEEP:, :] = fresh[slot * TOK : (slot + 1) * TOK]
    fk[mine] = fresh[0:TOK]
    c_f = [
        remote(kvb.at[slot, pl.ds(KEEP, TOK), :], fk.at[mine], dev) for slot, dev, _ in homeward
    ]

    q_lane = lax.broadcasted_iota(jnp.int32, (TOK, WIN), 1)
    for c in c_kv:
        c.wait_recv()
    for slot in range(GROUPS):
        q = qkv[slot * TOK : (slot + 1) * TOK, 0:WIN]
        spread = jnp.concatenate(
            [
                jnp.where((q_lane >= a * HEAD) & (q_lane < (a + 1) * HEAD), q, 0.0)
                for a in range(HEADS // GROUPS)
            ],
            axis=0,
        ).astype(BF16)
        scores = lax.dot_general(
            spread, kvb[slot, :, 0:WIN], (((1,), (1,)), ((), ())), preferred_element_type=F32
        ) * HEAD ** (-0.5)
        raised = jnp.exp(scores - jnp.max(scores, axis=-1, keepdims=True))
        probs = (raised / jnp.sum(raised, axis=-1, keepdims=True)).astype(BF16)
        mixed = jnp.dot(probs, kvb[slot, :, 256:KVW], preferred_element_type=F32)
        picked = jnp.zeros((TOK, WIN), F32)
        for a in range(HEADS // GROUPS):
            low = TOK + a * HEAD
            picked = jnp.where(
                (q_lane >= low) & (q_lane < low + HEAD), mixed[a * TOK : (a + 1) * TOK], picked
            )
        attn_v[slot * TOK : (slot + 1) * TOK, :] = picked.astype(BF16)

    c_wo.wait()
    for c in c_w:
        c.wait_recv()
    attn = attn_v[...]
    partial = jnp.concatenate(
        [jnp.dot(attn, wo_v[j], preferred_element_type=F32) for j in range(GROUPS)], axis=1
    )
    for slot in range(1, GROUPS):
        ps[slot - 1] = partial[slot * TOK : (slot + 1) * TOK].astype(BF16)
    c_p = [remote(ps.at[slot - 1], r2.at[i - 1], dev) for slot, dev, i in homeward]

    for c in c_f:
        c.wait_recv()
    for j in range(GROUPS):
        block = fk[j].astype(F32)
        fk_k = block[:, 0:BW]
        fk_v = block[:, BW : 2 * BW]
        if j == 0:
            keys, vals = [fk_k], [fk_v]
        else:
            keys.append(fk_k)
            vals.append(fk_v)
    fresh_out[...] = jnp.concatenate(keys + vals, axis=1).astype(BF16)
    c_fw.wait()
    channels = fw_v.shape[1]
    spots = (TOK // 2) * channels
    tile_row = lax.broadcasted_iota(jnp.int32, (channels, spots), 0)
    tile_col = lax.broadcasted_iota(jnp.int32, (channels, spots), 1)
    copies = (lax.rem(tile_col, channels) == tile_row).astype(BF16)
    fw_tiled = jnp.dot(fw_v[...], copies, preferred_element_type=F32).astype(BF16)

    for c in c_p:
        c.wait_recv()
    proj = partial[0:TOK]
    for i in range(GROUPS - 1):
        proj = proj + r2[i].astype(F32)
    h1 = h_v[...].astype(F32) + mod_v[2:3, :] * proj
    middle = layer_norm(h1) * (1.0 + mod_v[4:5, :]) + mod_v[3:4, :]
    x2[0] = middle.astype(BF16)
    c_m = [remote(x2.at[0], x2.at[slot], dev) for dev, _, slot in outward]
    c_wu.wait()
    c_wd.wait()
    for c in c_m:
        c.wait_recv()
    inner_v[...] = jax.nn.gelu(
        jnp.dot(x2[...].reshape(GROUPS * TOK, D), wu_v[...], preferred_element_type=F32),
        approximate=True,
    ).astype(BF16)
    part = jnp.dot(inner_v[...], wd_v[...], preferred_element_type=F32)
    for slot in range(1, GROUPS):
        parts[slot - 1] = part[slot * TOK : (slot + 1) * TOK].astype(BF16)
    c_d = [remote(parts.at[slot - 1], r4.at[i - 1], dev) for slot, dev, i in homeward]
    for c in c_d:
        c.wait_recv()
    total = part[0:TOK]
    for i in range(GROUPS - 1):
        total = total + r4[i].astype(F32)
    layer_out = (h1 + mod_v[5:6, :] * total).astype(BF16)

    half = TOK // 2
    upper = layer_out[:half]
    lower = layer_out[half:]
    first = s == 0
    leave[...] = jnp.where(first, lower, upper)
    c_a = remote(leave, arrive, other)
    c_fm.wait()
    c_nz.wait()
    c_a.wait_recv()
    arrived = arrive[...]
    next_out[...] = jnp.where(first, upper, arrived)
    final_rows = jnp.where(first, arrived, lower).astype(F32)
    shifted = (layer_norm(final_rows) * (1.0 + fmod_v[1:2, :]) + fmod_v[0:1, :]).astype(BF16)
    each = jnp.dot(shifted, fw_tiled, preferred_element_type=F32)
    row = lax.broadcasted_iota(jnp.int32, (half, spots), 0)
    col = lax.broadcasted_iota(jnp.int32, (half, spots), 1)
    noise = jnp.sum(jnp.where(lax.div(col, channels) == row, each, 0.0), axis=0, keepdims=True)
    now = jnp.full((1, spots), time_ref[0], jnp.int32)
    before = jnp.full((1, spots), time_ref[0] - gap_ref[0], jnp.int32)
    now_bar = alpha_bar(now.astype(F32))
    prev_bar = alpha_bar(before.astype(F32))
    clean = (noisy_v[...] - jnp.sqrt(1.0 - now_bar) * noise) / jnp.sqrt(now_bar)
    noise_out[...] = noise
    den_out[...] = jnp.sqrt(prev_bar) * clean + jnp.sqrt(1.0 - prev_bar) * noise

    for c in sends:
        c.wait_send()


def per_device(
    section_in,
    patch_index,
    stale_kv,
    modulation,
    final_mod,
    qkv_blocks,
    out_blocks,
    up_blocks,
    down_blocks,
    final_weight,
    noisy_latent,
    time_index,
    time_gap,
):
    any_spec = pl.BlockSpec(memory_space=pl.ANY)
    smem = pl.BlockSpec(memory_space=pltpu.SMEM)
    vmem = pl.BlockSpec(memory_space=pltpu.VMEM)
    spots = noisy_latent.shape[1]
    remote_count = 22
    fresh, next_rows, noise_pred, denoised = pl.pallas_call(
        kernel,
        name="relay_step",
        out_shape=(
            jax.ShapeDtypeStruct((TOK, 2 * D), BF16),
            jax.ShapeDtypeStruct((TOK // 2, D), BF16),
            jax.ShapeDtypeStruct((1, spots), F32),
            jax.ShapeDtypeStruct((1, spots), F32),
        ),
        in_specs=[smem] * 3 + [any_spec] * 10,
        out_specs=(vmem,) * 4,
        scratch_shapes=[
            pltpu.VMEM((TOK, D), BF16),
            pltpu.VMEM((4 * TOK, 2 * D), BF16),
            pltpu.VMEM((6, D), F32),
            pltpu.VMEM((2, D), F32),
            pltpu.VMEM((D, 3 * BW), BF16),
            pltpu.VMEM((GROUPS, WIN, BW), BF16),
            pltpu.VMEM((D, D), BF16),
            pltpu.VMEM((D, D), BF16),
            pltpu.VMEM(final_weight.shape, BF16),
            pltpu.VMEM((1, spots), F32),
            pltpu.VMEM((GROUPS, TOK, D), BF16),
            pltpu.VMEM((GROUPS, TOK, D), BF16),
            pltpu.VMEM((GROUPS, KEEP, KVW), BF16),
            pltpu.VMEM((GROUPS, KEEP + TOK, KVW), BF16),
            pltpu.VMEM((GROUPS, TOK, KVW), BF16),
            pltpu.VMEM((GROUPS * TOK, WIN), BF16),
            pltpu.VMEM((GROUPS * TOK, D), BF16),
            pltpu.VMEM((GROUPS - 1, TOK, D), BF16),
            pltpu.VMEM((GROUPS - 1, TOK, D), BF16),
            pltpu.VMEM((GROUPS - 1, TOK, D), BF16),
            pltpu.VMEM((GROUPS - 1, TOK, D), BF16),
            pltpu.VMEM((TOK // 2, D), BF16),
            pltpu.VMEM((TOK // 2, D), BF16),
            pltpu.SemaphoreType.DMA((10,)),
            pltpu.SemaphoreType.DMA((remote_count,)),
            pltpu.SemaphoreType.DMA((remote_count,)),
        ],
        compiler_params=pltpu.CompilerParams(
            collective_id=0, has_side_effects=True, vmem_limit_bytes=48 * 1024 * 1024
        ),
    )(
        patch_index,
        time_index,
        time_gap,
        section_in[0, 0],
        stale_kv[0, 0],
        modulation[0, 0],
        final_mod[0],
        qkv_blocks[0, 0],
        out_blocks[0, 0],
        up_blocks[0, 0],
        down_blocks[0, 0],
        final_weight,
        noisy_latent,
    )
    return (fresh[None, None], next_rows[None], noise_pred, denoised)


def solution(mesh):
    placed = (
        P("section", "req", None, None),
        P("section", "req"),
        P("section", "req", None, None),
        P("section", "req", None, None),
        P("req", None, None),
        P("section", "req", None, None),
        P("section", "req", None, None),
        P("section", "req", None, None),
        P("section", "req", None, None),
        P(),
        P("req", "section"),
        P("req"),
        P("req"),
    )
    return jax.shard_map(
        per_device,
        mesh=mesh,
        in_specs=placed,
        out_specs=(
            P("section", "req", None, None),
            P("req", "section", None),
            P("req", "section"),
            P("req", "section"),
        ),
        check_vma=False,
    )
```

time: 199 us -> 62.8 us (0.32)
  blocking collectives: 86.7 us -> 0 us
  Pallas kernels: 0 us -> 50.2 us
  waiting for transfers between devices: 24.5 us -> 0 us
  other arithmetic: 23.4 us -> 0 us
  starting transfers between devices: 22 us -> 0 us
  local copies, waits for them, and re-layouts: 28.8 us -> 9.64 us
  matrix products: 8.92 us -> 0 us
    all_to_all x4 -> x0, blocking collectives: 86.7 us -> none  [the longest x3 69.8 us: spread_regroup(): lax.all_to_all(outgoing, 'req', split_axis=0, concat_axis=0, tiled=True)]
    pallas_call x0 -> x1, Pallas kernels: none -> 50.2 us  [per_device(): pl.pallas_call(kernel, name='relay_step', out_shape=(jax.ShapeDtypeStruct...]
    all_to_all x2 -> x0, waiting for transfers between devices: 24.5 us -> none  [spread_regroup(): lax.all_to_all(block_fn(lax.all_to_all(outgoing, 'req', split_axis=0, con...]
    all_to_all x2 -> x0, starting transfers between devices: 14.2 us -> none  [spread_regroup(): lax.all_to_all(block_fn(lax.all_to_all(outgoing, 'req', split_axis=0, con...]
    dot_general x6 -> x0, matrix products: 8.92 us -> none  [the longest x2 3.67 us: block_product(): jnp.einsum('nsd,dc->nsc', incoming, weight, preferred_element_type=jnp.fl...]
    broadcast_in_dim x4 -> x0, other arithmetic: 8.6 us -> none  [the longest x3 7.97 us: spread_regroup(): jnp.broadcast_to(pieces[:, None], (slices, UNIT_GROUPS, per_slice, feature))]
    ppermute x1 -> x0, starting transfers between devices: 7.83 us -> none  [from_partner(): lax.ppermute(x, axis, [(i, i ^ 1 << bit) for i in range(lax.axis_size(axi...]
    convert_element_type x8 -> x0, other arithmetic: 7.26 us -> none  [the longest x1 2.45 us: layer_step(): total = jnp.sum(parts.astype(jnp.float32), axis=1)]
  transfers between devices with their start and end apart: 3 -> 0, of which waited for: 2 -> 0; matrix products, arithmetic and copies ran while one was open for 0% -> 0% of each run, Pallas kernels for 0% -> 0%
where the time goes in v1:
time: 62.8 us; the launch traced here: 62.4 us
  Pallas kernels  50.2 us (80%)
  local copies, waits for them, and re-layouts  9.64 us (15%)
  between operations  2.65 us (4%)
    pallas_call x1, Pallas kernels, per_device(): pl.pallas_call(kernel, name='relay_step', out_shape=(jax.ShapeDtypeStruct...  50.2 us
    unnamed x16, local copies, waits for them, and re-layouts  9.64 us

profile of v1, /device:TPU:1, one launch (start us, length us, event | category | flops | bytes accessed | tf_op | source)
XLA Modules:
  0.0 62.4 jit_solution(18022253663122843884)
XLA Ops:
  2.6 0.8 %copy.22 = f32[1,1,6,1152]{3,2,1,0:T(8,128)S(1)} copy(f32[1,1,6,1152]{3,1,2,0:T(1,128)} %param.16) | data formatting | bytes 55296
  3.3 1.0 %copy.19.fw_hbm = bf16[1152,16]{1,0:T(8,128)(2,1)S(1)} copy(bf16[1152,16]{0,1:T(8,128)(2,1)} %param.22) | data formatting | bytes 73728 | tf_op args[9]
  4.3 0.0 copy-start.1
  4.3 0.0 copy-start.2
  4.3 0.0 copy-start.3
  4.3 1.5 %copy.18 = bf16[1,1,1152,288]{3,2,1,0:T(8,128)(2,1)S(1)} copy(bf16[1,1,1152,288]{2,3,1,0:T(8,128)(2,1)} %param.19) | data formatting | bytes 1327104 | tf_op args[6]
  5.9 2.9 %copy.17 = bf16[1,1,1152,864]{3,2,1,0:T(8,128)(2,1)S(1)} copy(bf16[1,1,1152,864]{2,3,1,0:T(8,128)(2,1)} %param.18) | data formatting | bytes 3981312 | tf_op args[5]
  8.8 0.0 copy-done.1
  8.8 0.0 copy-done.2
  8.8 0.0 copy-done.3
  8.8 0.0 copy-start
  8.8 1.1 %copy-done = bf16[1,1,128,2304]{3,2,1,0:T(8,128)(2,1)S(1)} copy-done((bf16[1,1,128,2304]{3,2,1,0:T(8,128)(2,1)S(1)}, bf16[1,1,128,2304]{3,2,1,0:T(8,128)(2,1)}, u32[]{:S(2)}) %copy-start) | copy-done | bytes 589848
  9.9 50.2 %relay_step.1 = (bf16[32,2304]{1,0:T(8,128)(2,1)S(1)}, bf16[16,1152]{1,0:T(8,128)(2,1)S(1)}, f32[1,256]{1,0:T(1,128)S(1)}, f32[1,256]{1,0:T(1,128)S(1)}) custom-call(s32[1,1]{1,0:T(1,128)S(6)} %copy.27.patch_ref, s32[1]{0:T(128)S(6)} %copy.28.time_ref, s32[1]{0:T(128)S(6)} %copy.29.gap_ref, bf16[32,1152]{1,0:T(8,128)(2,1)S(1)} %bitcast.17, ...), custom_call_target="tpu_custom_call" | custom-call | tf_op jit(solution)/shard_map/relay_step/pallas_call | solution.py:333
  60.0 0.7 %copy.30 = bf16[1,1,32,2304]{3,2,1,0:T(8,128)(2,1)} copy(bf16[1,1,32,2304]{3,2,1,0:T(8,128)(2,1)S(1)} %bitcast.16) | data formatting | bytes 294912
  60.7 0.6 copy.31
  61.3 0.6 copy.32
  61.9 0.6 copy.33
Async XLA Ops:
  4.3 4.5 %copy-start.1 = (bf16[1,1,32,1152]{3,2,1,0:T(8,128)(2,1)S(1)}, bf16[1,1,32,1152]{3,2,1,0:T(8,128)(2,1)}, u32[]{:S(2)}) copy-start(bf16[1,1,32,1152]{3,2,1,0:T(8,128)(2,1)} %param.13) | copy-start | bytes 221188
  4.3 4.5 %copy-start.2 = (f32[1,2,1152]{2,1,0:T(2,128)S(1)}, f32[1,2,1152]{2,1,0:T(2,128)}, u32[]{:S(2)}) copy-start(f32[1,2,1152]{2,1,0:T(2,128)} %param.17) | copy-start | bytes 27652
  4.3 4.5 %copy-start.3 = (f32[1,256]{1,0:T(1,128)S(1)}, f32[1,256]{1,0:T(1,128)}, u32[]{:S(2)}) copy-start(f32[1,256]{1,0:T(1,128)} %noisy_hbm.1) | copy-start | bytes 3076
  8.8 1.1 %copy-start = (bf16[1,1,128,2304]{3,2,1,0:T(8,128)(2,1)S(1)}, bf16[1,1,128,2304]{3,2,1,0:T(8,128)(2,1)}, u32[]{:S(2)}) copy-start(bf16[1,1,128,2304]{3,2,1,0:T(8,128)(2,1)} %param.15) | copy-start | bytes 1769476

commit v2 on v1

--- a/solution.py
+++ b/solution.py
@@ -32,6 +32,10 @@
     return centred * lax.rsqrt(spread + NORM_EPS)
 
 
+def dot_t(a, b):
+    return lax.dot_general(a, b, (((1,), (1,)), ((), ())), preferred_element_type=F32)
+
+
 def alpha_bar(moment):
     return jnp.exp(
         -(BETA_LOW * (moment + 1.0) + (BETA_HIGH - BETA_LOW) * moment * (moment + 1.0) / 1998.0)
@@ -39,9 +43,9 @@
 
 
 def kernel(
-    patch_ref,
-    time_ref,
-    gap_ref,
+    patch_hbm,
+    time_hbm,
+    gap_hbm,
     h_hbm,
     stale_hbm,
     mod_hbm,
@@ -56,6 +60,9 @@
     next_out,
     noise_out,
     den_out,
+    patch_ref,
+    time_ref,
+    gap_ref,
     h_v,
     st_v,
     mod_v,
@@ -113,20 +120,24 @@
     c_h = load(0, h_hbm, h_v)
     c_mod = load(1, mod_hbm, mod_v)
     c_st = load(2, stale_hbm, st_v)
+    c_pt = load(10, patch_hbm, patch_ref)
     c_wq = load(3, wq_hbm, wq_v)
 
     barrier = pltpu.get_barrier_semaphore()
     for peer in (at(1), at(-1), at(2), at(-2), other):
         pl.semaphore_signal(barrier, inc=1, device_id=peer, device_id_type=MESH)
 
-    wo_v[:, 0:TOK, :] = jnp.zeros((GROUPS, TOK, BW), BF16)
-    wo_v[:, TOK + BW :, :] = jnp.zeros((GROUPS, WIN - TOK - BW, BW), BF16)
-    c_wo = load(4, wo_hbm.at[pl.ds(mine * BW, BW), :], wo_v.at[mine, pl.ds(TOK, BW), :])
+    def heads_rows(j):
+        return wo_hbm.at[:, pl.ds(pl.multiple_of(j * 256, 256), WIN)]
+
+    c_wo = load(4, heads_rows(mine), wo_v.at[mine])
     c_wu = load(5, wu_hbm, wu_v)
     c_wd = load(6, wd_hbm, wd_v)
     c_fw = load(7, fw_hbm, fw_v)
     c_fm = load(8, fmod_hbm, fmod_v)
     c_nz = load(9, noisy_hbm, noisy_v)
+    c_tm = load(11, time_hbm, time_ref)
+    c_gp = load(12, gap_hbm, gap_ref)
 
     sends = []
     count = [0]
@@ -148,10 +159,11 @@
 
     c_h.wait()
     c_mod.wait()
-    normed = layer_norm(h_v[...].astype(F32)) * (1.0 + mod_v[1:2, :]) + mod_v[0:1, :]
+    normed = layer_norm(h_v[...].astype(F32)) * (1.0 + mod_v[1]) + mod_v[0]
     x1[0] = normed.astype(BF16)
 
     c_st.wait()
+    c_pt.wait()
     patch = patch_ref[0, 0]
     for k in range(3):
         low = st_v[k * TOK : (k + 1) * TOK, :].astype(F32)
@@ -174,18 +186,14 @@
         remote(kvs.at[res], kvb.at[slot, pl.ds(0, KEEP), :], dev) for dev, res, slot in outward
     ]
     c_w = [
-        remote(
-            wo_hbm.at[pl.ds(res * BW, BW), :],
-            wo_v.at[mine, pl.ds(TOK, BW), :],
-            dev,
-        )
+        remote(heads_rows(res), wo_v.at[mine], dev)
         for dev, res, _ in outward
     ]
 
     c_wq.wait()
     for c in c_x:
         c.wait_recv()
-    qkv = jnp.dot(x1[...].reshape(GROUPS * TOK, D), wq_v[...], preferred_element_type=F32)
+    qkv = dot_t(x1[...].reshape(GROUPS * TOK, D), wq_v[...])
     fresh = jnp.concatenate(
         [qkv[:, BW:], jnp.zeros((GROUPS * TOK, KVW - 2 * BW), F32)], axis=1
     ).astype(BF16)
@@ -208,9 +216,7 @@
             ],
             axis=0,
         ).astype(BF16)
-        scores = lax.dot_general(
-            spread, kvb[slot, :, 0:WIN], (((1,), (1,)), ((), ())), preferred_element_type=F32
-        ) * HEAD ** (-0.5)
+        scores = dot_t(spread, kvb[slot, :, 0:WIN]) * HEAD ** (-0.5)
         raised = jnp.exp(scores - jnp.max(scores, axis=-1, keepdims=True))
         probs = (raised / jnp.sum(raised, axis=-1, keepdims=True)).astype(BF16)
         mixed = jnp.dot(probs, kvb[slot, :, 256:KVW], preferred_element_type=F32)
@@ -220,14 +226,15 @@
             picked = jnp.where(
                 (q_lane >= low) & (q_lane < low + HEAD), mixed[a * TOK : (a + 1) * TOK], picked
             )
-        attn_v[slot * TOK : (slot + 1) * TOK, :] = picked.astype(BF16)
+        shift = lax.rem(TOK * (mine + WIN // TOK - 1), WIN)
+        attn_v[slot * TOK : (slot + 1) * TOK, :] = pltpu.roll(picked, shift, 1).astype(BF16)
 
     c_wo.wait()
     for c in c_w:
         c.wait_recv()
     attn = attn_v[...]
     partial = jnp.concatenate(
-        [jnp.dot(attn, wo_v[j], preferred_element_type=F32) for j in range(GROUPS)], axis=1
+        [dot_t(attn, wo_v[j]) for j in range(GROUPS)], axis=1
     )
     for slot in range(1, GROUPS):
         ps[slot - 1] = partial[slot * TOK : (slot + 1) * TOK].astype(BF16)
@@ -246,20 +253,17 @@
             vals.append(fk_v)
     fresh_out[...] = jnp.concatenate(keys + vals, axis=1).astype(BF16)
     c_fw.wait()
-    channels = fw_v.shape[1]
+    channels = fw_v.shape[0]
     spots = (TOK // 2) * channels
-    tile_row = lax.broadcasted_iota(jnp.int32, (channels, spots), 0)
-    tile_col = lax.broadcasted_iota(jnp.int32, (channels, spots), 1)
-    copies = (lax.rem(tile_col, channels) == tile_row).astype(BF16)
-    fw_tiled = jnp.dot(fw_v[...], copies, preferred_element_type=F32).astype(BF16)
+    fw_tiled = jnp.concatenate([fw_v[...]] * (TOK // 2), axis=0)
 
     for c in c_p:
         c.wait_recv()
     proj = partial[0:TOK]
     for i in range(GROUPS - 1):
         proj = proj + r2[i].astype(F32)
-    h1 = h_v[...].astype(F32) + mod_v[2:3, :] * proj
-    middle = layer_norm(h1) * (1.0 + mod_v[4:5, :]) + mod_v[3:4, :]
+    h1 = h_v[...].astype(F32) + mod_v[2] * proj
+    middle = layer_norm(h1) * (1.0 + mod_v[4]) + mod_v[3]
     x2[0] = middle.astype(BF16)
     c_m = [remote(x2.at[0], x2.at[slot], dev) for dev, _, slot in outward]
     c_wu.wait()
@@ -279,7 +283,7 @@
     total = part[0:TOK]
     for i in range(GROUPS - 1):
         total = total + r4[i].astype(F32)
-    layer_out = (h1 + mod_v[5:6, :] * total).astype(BF16)
+    layer_out = (h1 + mod_v[5] * total).astype(BF16)
 
     half = TOK // 2
     upper = layer_out[:half]
@@ -289,12 +293,14 @@
     c_a = remote(leave, arrive, other)
     c_fm.wait()
     c_nz.wait()
+    c_tm.wait()
+    c_gp.wait()
     c_a.wait_recv()
     arrived = arrive[...]
     next_out[...] = jnp.where(first, upper, arrived)
     final_rows = jnp.where(first, arrived, lower).astype(F32)
     shifted = (layer_norm(final_rows) * (1.0 + fmod_v[1:2, :]) + fmod_v[0:1, :]).astype(BF16)
-    each = jnp.dot(shifted, fw_tiled, preferred_element_type=F32)
+    each = dot_t(shifted, fw_tiled)
     row = lax.broadcasted_iota(jnp.int32, (half, spots), 0)
     col = lax.broadcasted_iota(jnp.int32, (half, spots), 1)
     noise = jnp.sum(jnp.where(lax.div(col, channels) == row, each, 0.0), axis=0, keepdims=True)
@@ -325,8 +331,7 @@
     time_index,
     time_gap,
 ):
-    any_spec = pl.BlockSpec(memory_space=pl.ANY)
-    smem = pl.BlockSpec(memory_space=pltpu.SMEM)
+    any_spec = pl.BlockSpec(memory_space=pltpu.HBM)
     vmem = pl.BlockSpec(memory_space=pltpu.VMEM)
     spots = noisy_latent.shape[1]
     remote_count = 22
@@ -339,18 +344,21 @@
             jax.ShapeDtypeStruct((1, spots), F32),
             jax.ShapeDtypeStruct((1, spots), F32),
         ),
-        in_specs=[smem] * 3 + [any_spec] * 10,
+        in_specs=[any_spec] * 13,
         out_specs=(vmem,) * 4,
         scratch_shapes=[
+            pltpu.SMEM((1, 1), jnp.int32),
+            pltpu.SMEM((1,), jnp.int32),
+            pltpu.SMEM((1,), jnp.int32),
             pltpu.VMEM((TOK, D), BF16),
             pltpu.VMEM((4 * TOK, 2 * D), BF16),
-            pltpu.VMEM((6, D), F32),
+            pltpu.VMEM((6, 1, D), F32),
             pltpu.VMEM((2, D), F32),
-            pltpu.VMEM((D, 3 * BW), BF16),
-            pltpu.VMEM((GROUPS, WIN, BW), BF16),
+            pltpu.VMEM((3 * BW, D), BF16),
+            pltpu.VMEM((GROUPS, BW, WIN), BF16),
             pltpu.VMEM((D, D), BF16),
             pltpu.VMEM((D, D), BF16),
-            pltpu.VMEM(final_weight.shape, BF16),
+            pltpu.VMEM(final_weight.shape[::-1], BF16),
             pltpu.VMEM((1, spots), F32),
             pltpu.VMEM((GROUPS, TOK, D), BF16),
             pltpu.VMEM((GROUPS, TOK, D), BF16),
@@ -365,12 +373,12 @@
             pltpu.VMEM((GROUPS - 1, TOK, D), BF16),
             pltpu.VMEM((TOK // 2, D), BF16),
             pltpu.VMEM((TOK // 2, D), BF16),
-            pltpu.SemaphoreType.DMA((10,)),
+            pltpu.SemaphoreType.DMA((13,)),
             pltpu.SemaphoreType.DMA((remote_count,)),
             pltpu.SemaphoreType.DMA((remote_count,)),
         ],
         compiler_params=pltpu.CompilerParams(
-            collective_id=0, has_side_effects=True, vmem_limit_bytes=48 * 1024 * 1024
+            collective_id=0, has_side_effects=True, vmem_limit_bytes=63 * 1024 * 1024
         ),
     )(
         patch_index,
@@ -378,13 +386,13 @@
         time_gap,
         section_in[0, 0],
         stale_kv[0, 0],
-        modulation[0, 0],
+        modulation[0, 0][:, None, :],
         final_mod[0],
-        qkv_blocks[0, 0],
-        out_blocks[0, 0],
+        qkv_blocks[0, 0].T,
+        out_blocks[0, 0].T,
         up_blocks[0, 0],
         down_blocks[0, 0],
-        final_weight,
+        final_weight.T,
         noisy_latent,
     )
     return (fresh[None, None], next_rows[None], noise_pred, denoised)

time: 62.8 us -> 58.4 us (0.930)
  local copies, waits for them, and re-layouts: 9.64 us -> 5.34 us
    unnamed x16 -> x4, local copies, waits for them, and re-layouts: 9.64 us -> 5.34 us
where the time goes in v2:
time: 58.4 us; the launch traced here: 58.2 us
  Pallas kernels  50.2 us (86%)
  local copies, waits for them, and re-layouts  5.34 us (9%)
  between operations  2.58 us (4%)
    pallas_call x1, Pallas kernels, per_device(): pl.pallas_call(kernel, name='relay_step', out_shape=(jax.ShapeDtypeStruct...  50.2 us
    unnamed x4, local copies, waits for them, and re-layouts  5.34 us

profile of v2, /device:TPU:1, one launch (start us, length us, event | category | flops | bytes accessed | tf_op | source)
XLA Modules:
  0.0 58.2 jit_solution(8574454397072930902)
XLA Ops:
  2.6 50.2 %relay_step.1 = (bf16[32,2304]{1,0:T(8,128)(2,1)}, bf16[16,1152]{1,0:T(8,128)(2,1)}, f32[1,256]{1,0:T(1,128)}, f32[1,256]{1,0:T(1,128)}) custom-call(s32[1,1]{1,0:T(1,128)S(6)} %copy.21.patch_hbm, s32[1]{0:T(128)S(6)} %copy.22.time_hbm, s32[1]{0:T(128)S(6)} %copy.23.gap_hbm, bf16[32,1152]{1,0:T(8,128)(2,1)} %bitcast.21, bf16[128,2304]{1,0:T(8,128)(2,1)} %bitcast.19, ...), custom_call_target="tpu_custom_call" | custom-call | tf_op jit(solution)/shard_map/relay_step/pallas_call | solution.py:338
  52.8 1.6 %copy.24 = bf16[1,1,32,2304]{3,2,1,0:T(8,128)(2,1)} copy(bf16[1,1,32,2304]{3,2,1,0:T(8,128)(2,1)} %bitcast.20) | data formatting | bytes 294912
  54.4 1.4 %copy.25 = bf16[1,16,1152]{2,1,0:T(8,128)(2,1)} copy(bf16[1,16,1152]{2,1,0:T(8,128)(2,1)} %bitcast.23) | data formatting | bytes 73728
  55.8 1.2 %copy.26 = f32[1,256]{1,0:T(1,128)} copy(f32[1,256]{1,0:T(1,128)} %get-tuple-element.18) | data formatting | bytes 2048
  57.0 1.2 %copy.27 = f32[1,256]{1,0:T(1,128)} copy(f32[1,256]{1,0:T(1,128)} %get-tuple-element.19) | data formatting | bytes 2048

commit v3 on v2

v3 whole, which is shorter than its diff:
```python
import functools

import jax
import jax.numpy as jnp
from jax import lax
from jax.experimental import pallas as pl
from jax.experimental.pallas import tpu as pltpu
from jax.sharding import PartitionSpec as P

MESH = pl.DeviceIdType.MESH
HEADS = 16
GROUPS = 4
NORM_EPS = 1e-06
BETA_LOW = 0.0001
BETA_HIGH = 0.02
TOK = 32
HALF = TOK // 2
D = 1152
BW = D // GROUPS
HEAD = D // HEADS
KEEP = 96
WIN = 384
RING = 8
F32 = jnp.float32
BF16 = jnp.bfloat16


def layer_norm(values):
    average = jnp.mean(values, axis=-1, keepdims=True)
    centred = values - average
    spread = jnp.mean(centred * centred, axis=-1, keepdims=True)
    return centred * lax.rsqrt(spread + NORM_EPS)


def dot_t(a, b):
    return lax.dot_general(a, b, (((1,), (1,)), ((), ())), preferred_element_type=F32)


def alpha_bar(moment):
    return jnp.exp(
        -(BETA_LOW * (moment + 1.0) + (BETA_HIGH - BETA_LOW) * moment * (moment + 1.0) / 1998.0)
    )


def kernel(
    patch_hbm,
    time_hbm,
    gap_hbm,
    h_hbm,
    stale_hbm,
    mod_hbm,
    fmod_hbm,
    wq_hbm,
    wo_hbm,
    wu_hbm,
    wd_hbm,
    fw_hbm,
    noisy_hbm,
    fresh_out,
    next_out,
    noise_out,
    den_out,
    patch_ref,
    time_ref,
    gap_ref,
    h_v,
    st_v,
    mod_v,
    fmod_v,
    wq_v,
    wo_v,
    wu_v,
    wd_v,
    fw_v,
    noisy_v,
    x1,
    qs,
    qr,
    kv,
    x2,
    ps,
    pr,
    x3,
    inner_v,
    parts,
    r4,
    leave,
    arrive,
    lsem,
    ssem,
    rsem,
):
    s = lax.axis_index("section")
    r = lax.axis_index("req")
    z = lax.rem(r, RING)
    base = r - z
    odd = lax.rem(z, 2)
    mine = lax.rem(z, GROUPS)

    def at(dz):
        return (s, base + lax.rem(z + dz + RING, RING))

    far = 2 - 4 * odd
    outward = [(at(far), 3), (at(1), 2), (at(-1), 1)]
    homeward = [(3, at(-far), 3), (1, at(1), 2), (2, at(-1), 1)]
    other = (1 - s, r)
    rows = [pl.multiple_of(HALF * (1 - s), HALF), pl.multiple_of(HALF * s, HALF)]
    halves = (0, 1)

    local = []

    def load(i, src, dst):
        copy = pltpu.make_async_copy(src, dst, lsem.at[i])
        copy.start()
        local.append(copy)
        return copy

    c_h = load(0, h_hbm, h_v)
    c_mod = load(1, mod_hbm, mod_v)
    barrier = pltpu.get_barrier_semaphore()
    for peer in (at(1), at(-1), at(2), at(-2), other):
        pl.semaphore_signal(barrier, inc=1, device_id=peer, device_id_type=MESH)
    c_wq = load(3, wq_hbm, wq_v)
    c_pt = load(10, patch_hbm, patch_ref)
    c_st = load(2, stale_hbm, st_v)
    c_wo = load(4, wo_hbm, wo_v)
    c_wu = load(5, wu_hbm, wu_v)
    c_wd = load(6, wd_hbm, wd_v)
    c_fw = load(7, fw_hbm, fw_v)
    c_fm = load(8, fmod_hbm, fmod_v)
    c_nz = load(9, noisy_hbm, noisy_v)
    c_tm = load(11, time_hbm, time_ref)
    c_gp = load(12, gap_hbm, gap_ref)

    sends = []
    count = [0]

    def remote(src, dst, device):
        i = count[0]
        count[0] += 1
        copy = pltpu.make_async_remote_copy(
            src_ref=src,
            dst_ref=dst,
            send_sem=ssem.at[i],
            recv_sem=rsem.at[i],
            device_id=device,
            device_id_type=MESH,
        )
        copy.start()
        sends.append(copy)
        return copy

    def spread_tokens(buf, o):
        return [remote(buf.at[o, 0], buf.at[o, slot], dev) for dev, slot in outward]

    def arrive_all(copies):
        for c in copies:
            c.wait_recv()

    c_h.wait()
    c_mod.wait()
    normed = layer_norm(h_v[...].astype(F32)) * (1.0 + mod_v[1]) + mod_v[0]
    flip = s == 0
    x1[0, 0] = jnp.where(flip, normed[HALF:], normed[:HALF]).astype(BF16)
    x1[1, 0] = jnp.where(flip, normed[:HALF], normed[HALF:]).astype(BF16)

    pl.semaphore_wait(barrier, 5)
    c_x = [spread_tokens(x1, o) for o in halves]

    c_st.wait()
    c_pt.wait()
    patch = patch_ref[0, 0]
    for k in range(3):
        low = st_v[k * TOK : (k + 1) * TOK, :]
        high = st_v[(k + 1) * TOK : (k + 2) * TOK, :]
        kv[k * TOK : (k + 1) * TOK, :] = jnp.where(patch <= k, high, low)

    c_wq.wait()
    c_q = []
    for o in halves:
        arrive_all(c_x[o])
        qkv = dot_t(x1[o].reshape(GROUPS * HALF, D), wq_v[...]).astype(BF16)
        qs[o] = qkv.reshape(GROUPS, HALF, 3 * BW)
        c_q.append([remote(qs.at[o, slot], qr.at[o, mine], dev) for slot, dev, _ in homeward])
        qr[o, mine] = qkv[0:HALF]

    queries = []
    for o in halves:
        arrive_all(c_q[o])
        blocks = [qr[o, j].astype(F32) for j in range(GROUPS)]
        queries.append(jnp.concatenate([b[:, 0:BW] for b in blocks], axis=1))
        fresh = jnp.concatenate(
            [b[:, BW : 2 * BW] for b in blocks] + [b[:, 2 * BW :] for b in blocks], axis=1
        )
        kv[pl.ds(KEEP + rows[o], HALF), :] = fresh.astype(BF16)

    lane = lax.broadcasted_iota(jnp.int32, (HALF, WIN), 1)
    c_wo.wait()
    c_m = []
    for o in halves:
        wins = []
        for j in range(GROUPS):
            q = queries[o][:, 256 * j : 256 * j + WIN]
            masks = [
                (lane >= TOK * j + a * HEAD) & (lane < TOK * j + (a + 1) * HEAD)
                for a in range(HEADS // GROUPS)
            ]
            spread = jnp.concatenate([jnp.where(m, q, 0.0) for m in masks], axis=0).astype(BF16)
            scores = dot_t(spread, kv[:, 256 * j : 256 * j + WIN]) * HEAD ** (-0.5)
            raised = jnp.exp(scores - jnp.max(scores, axis=-1, keepdims=True))
            probs = (raised / jnp.sum(raised, axis=-1, keepdims=True)).astype(BF16)
            mixed = jnp.dot(
                probs, kv[:, D + 256 * j : D + 256 * j + WIN], preferred_element_type=F32
            )
            picked = jnp.zeros((HALF, WIN), F32)
            for a, m in enumerate(masks):
                picked = jnp.where(m, mixed[a * HALF : (a + 1) * HALF], picked)
            wins.append(picked)
        cuts = [wins[0][:, 0:256]]
        for j in range(1, GROUPS):
            cuts.append(wins[j - 1][:, 256:WIN] + wins[j][:, 0:128])
            cuts.append(wins[j][:, 128:256])
        cuts.append(wins[GROUPS - 1][:, 256:WIN])
        x2[o, 0] = jnp.concatenate(cuts, axis=1).astype(BF16)
        c_m.append(spread_tokens(x2, o))

    c_p = []
    for o in halves:
        arrive_all(c_m[o])
        proj = dot_t(x2[o].reshape(GROUPS * HALF, D), wo_v[...]).astype(BF16)
        ps[o] = proj.reshape(GROUPS, HALF, BW)
        c_p.append([remote(ps.at[o, slot], pr.at[o, mine], dev) for slot, dev, _ in homeward])
        pr[o, mine] = proj[0:HALF]

    c_u = []
    kept = []
    for o in halves:
        arrive_all(c_p[o])
        proj = jnp.concatenate([pr[o, j].astype(F32) for j in range(GROUPS)], axis=1)
        h1 = h_v[pl.ds(rows[o], HALF), :].astype(F32) + mod_v[2] * proj
        kept.append(h1)
        middle = layer_norm(h1) * (1.0 + mod_v[4]) + mod_v[3]
        x3[o, 0] = middle.astype(BF16)
        c_u.append(spread_tokens(x3, o))

    fresh_out[...] = kv[KEEP:, :]
    c_fw.wait()
    channels = fw_v.shape[0]
    spots = HALF * channels
    fw_tiled = jnp.concatenate([fw_v[...]] * HALF, axis=0)

    c_wu.wait()
    c_wd.wait()
    c_d = []
    own = []
    for o in halves:
        arrive_all(c_u[o])
        inner_v[...] = jax.nn.gelu(
            jnp.dot(x3[o].reshape(GROUPS * HALF, D), wu_v[...], preferred_element_type=F32),
            approximate=True,
        ).astype(BF16)
        part = jnp.dot(inner_v[...], wd_v[...], preferred_element_type=F32)
        own.append(part[0:HALF])
        parts[o] = part.astype(BF16).reshape(GROUPS, HALF, D)
        c_d.append(
            [remote(parts.at[o, slot], r4.at[o, i - 1], dev) for slot, dev, i in homeward]
        )

    outs = []
    for o in halves:
        arrive_all(c_d[o])
        total = own[o]
        for i in range(GROUPS - 1):
            total = total + r4[o, i].astype(F32)
        outs.append((kept[o] + mod_v[5] * total).astype(BF16))
        if o == 0:
            leave[...] = outs[0]
            c_a = remote(leave, arrive, other)

    c_fm.wait()
    c_nz.wait()
    c_tm.wait()
    c_gp.wait()
    c_a.wait_recv()
    arrived = arrive[...]
    next_out[...] = jnp.where(flip, outs[1], arrived)
    final_rows = jnp.where(flip, arrived, outs[1]).astype(F32)
    shifted = (layer_norm(final_rows) * (1.0 + fmod_v[1:2, :]) + fmod_v[0:1, :]).astype(BF16)
    each = dot_t(shifted, fw_tiled)
    row = lax.broadcasted_iota(jnp.int32, (HALF, spots), 0)
    col = lax.broadcasted_iota(jnp.int32, (HALF, spots), 1)
    noise = jnp.sum(jnp.where(lax.div(col, channels) == row, each, 0.0), axis=0, keepdims=True)
    now = jnp.full((1, spots), time_ref[0], jnp.int32)
    before = jnp.full((1, spots), time_ref[0] - gap_ref[0], jnp.int32)
    now_bar = alpha_bar(now.astype(F32))
    prev_bar = alpha_bar(before.astype(F32))
    clean = (noisy_v[...] - jnp.sqrt(1.0 - now_bar) * noise) / jnp.sqrt(now_bar)
    noise_out[...] = noise
    den_out[...] = jnp.sqrt(prev_bar) * clean + jnp.sqrt(1.0 - prev_bar) * noise

    for c in sends:
        c.wait_send()


def write_out(*refs):
    count = (len(refs) - 1) // 2
    sem = refs[-1]
    copies = [
        pltpu.make_async_copy(refs[i], refs[count + i], sem.at[i]) for i in range(count)
    ]
    for c in copies:
        c.start()
    for c in copies:
        c.wait()


def per_device(
    section_in,
    patch_index,
    stale_kv,
    modulation,
    final_mod,
    qkv_blocks,
    out_blocks,
    up_blocks,
    down_blocks,
    final_weight,
    noisy_latent,
    time_index,
    time_gap,
):
    any_spec = pl.BlockSpec(memory_space=pltpu.HBM)
    vmem = pl.BlockSpec(memory_space=pltpu.VMEM)
    spots = noisy_latent.shape[1]
    remote_count = 37
    outs = pl.pallas_call(
        kernel,
        name="relay_step",
        out_shape=(
            jax.ShapeDtypeStruct((TOK, 2 * D), BF16),
            jax.ShapeDtypeStruct((TOK // 2, D), BF16),
            jax.ShapeDtypeStruct((1, spots), F32),
            jax.ShapeDtypeStruct((1, spots), F32),
        ),
        in_specs=[any_spec] * 13,
        out_specs=(vmem,) * 4,
        scratch_shapes=[
            pltpu.SMEM((1, 1), jnp.int32),
            pltpu.SMEM((1,), jnp.int32),
            pltpu.SMEM((1,), jnp.int32),
            pltpu.VMEM((TOK, D), BF16),
            pltpu.VMEM((4 * TOK, 2 * D), BF16),
            pltpu.VMEM((6, 1, D), F32),
            pltpu.VMEM((2, D), F32),
            pltpu.VMEM((3 * BW, D), BF16),
            pltpu.VMEM((BW, D), BF16),
            pltpu.VMEM((D, D), BF16),
            pltpu.VMEM((D, D), BF16),
            pltpu.VMEM(final_weight.shape[::-1], BF16),
            pltpu.VMEM((1, spots), F32),
            pltpu.VMEM((2, GROUPS, HALF, D), BF16),
            pltpu.VMEM((2, GROUPS, HALF, 3 * BW), BF16),
            pltpu.VMEM((2, GROUPS, HALF, 3 * BW), BF16),
            pltpu.VMEM((KEEP + TOK, 2 * D), BF16),
            pltpu.VMEM((2, GROUPS, HALF, D), BF16),
            pltpu.VMEM((2, GROUPS, HALF, BW), BF16),
            pltpu.VMEM((2, GROUPS, HALF, BW), BF16),
            pltpu.VMEM((2, GROUPS, HALF, D), BF16),
            pltpu.VMEM((GROUPS * HALF, D), BF16),
            pltpu.VMEM((2, GROUPS, HALF, D), BF16),
            pltpu.VMEM((2, GROUPS - 1, HALF, D), BF16),
            pltpu.VMEM((HALF, D), BF16),
            pltpu.VMEM((HALF, D), BF16),
            pltpu.SemaphoreType.DMA((13,)),
            pltpu.SemaphoreType.DMA((remote_count,)),
            pltpu.SemaphoreType.DMA((remote_count,)),
        ],
        compiler_params=pltpu.CompilerParams(
            collective_id=0, has_side_effects=True, vmem_limit_bytes=48 * 1024 * 1024
        ),
    )(
        patch_index,
        time_index,
        time_gap,
        *(pltpu.with_memory_space_constraint(a, pltpu.HBM) for a in (        section_in[0, 0],
        stale_kv[0, 0],
        modulation[0, 0][:, None, :],
        final_mod[0],
        qkv_blocks[0, 0].T,
        out_blocks[0, 0].T,
        up_blocks[0, 0],
        down_blocks[0, 0],
        final_weight.T,
        noisy_latent,))
    )
    fresh, next_rows, noise_pred, denoised = pl.pallas_call(
        write_out,
        name="write_out",
        out_shape=tuple(jax.ShapeDtypeStruct(o.shape, o.dtype) for o in outs),
        in_specs=(vmem,) * 4,
        out_specs=(any_spec,) * 4,
        scratch_shapes=[pltpu.SemaphoreType.DMA((4,))],
    )(*(pltpu.with_memory_space_constraint(o, pltpu.VMEM) for o in outs))
    return (fresh[None, None], next_rows[None], noise_pred, denoised)


def solution(mesh):
    placed = (
        P("section", "req", None, None),
        P("section", "req"),
        P("section", "req", None, None),
        P("section", "req", None, None),
        P("req", None, None),
        P("section", "req", None, None),
        P("section", "req", None, None),
        P("section", "req", None, None),
        P("section", "req", None, None),
        P(),
        P("req", "section"),
        P("req"),
        P("req"),
    )
    return jax.shard_map(
        per_device,
        mesh=mesh,
        in_specs=placed,
        out_specs=(
            P("section", "req", None, None),
            P("req", "section", None),
            P("req", "section"),
            P("req", "section"),
        ),
        check_vma=False,
    )
```

time: 58.4 us -> 42.8 us (0.73)
  Pallas kernels: 50.2 us -> 40.1 us
  local copies, waits for them, and re-layouts: 5.34 us -> 0 us
    pallas_call x1, Pallas kernels: 50.2 us -> 39.4 us  [per_device(): pl.pallas_call(kernel, name='relay_step', out_shape=(jax.ShapeDtypeStruct...]
    unnamed x4 -> x0, local copies, waits for them, and re-layouts: 5.34 us -> none
    pallas_call x0 -> x1, Pallas kernels: none -> 0.71 us  [per_device(): pl.pallas_call(write_out, name='write_out', out_shape=tuple((jax.ShapeDty...]
where the time goes in v3:
time: 42.8 us; the launch traced here: 42.7 us
  Pallas kernels  40.1 us (94%)
  between operations  2.58 us (6%)
    pallas_call x1, Pallas kernels, per_device(): pl.pallas_call(kernel, name='relay_step', out_shape=(jax.ShapeDtypeStruct...  39.4 us

profile of v3, /device:TPU:1, one launch (start us, length us, event | category | flops | bytes accessed | tf_op | source)
XLA Modules:
  0.0 42.7 jit_solution(6311067236471117774)
XLA Ops:
  2.6 39.4 %relay_step.1 = (bf16[32,2304]{1,0:T(8,128)(2,1)S(1)}, bf16[16,1152]{1,0:T(8,128)(2,1)S(1)}, f32[1,256]{1,0:T(1,128)S(1)}, f32[1,256]{1,0:T(1,128)S(1)}) custom-call(s32[1,1]{1,0:T(1,128)S(6)} %copy.17.patch_hbm, s32[1]{0:T(128)S(6)} %copy.18.time_hbm, s32[1]{0:T(128)S(6)} %copy.19.gap_hbm, bf16[32,1152]{1,0:T(8,128)(2,1)} %bitcast.20, ...), custom_call_target="tpu_custom_call" | custom-call | tf_op jit(solution)/shard_map/relay_step/pallas_call | solution.py:336
  42.0 0.7 %write_out.1 = (bf16[32,2304]{1,0:T(8,128)(2,1)}, bf16[16,1152]{1,0:T(8,128)(2,1)}, f32[1,256]{1,0:T(1,128)}, f32[1,256]{1,0:T(1,128)}) custom-call(bf16[32,2304]{1,0:T(8,128)(2,1)S(1)} %get-tuple-element.12.refs_0_, bf16[16,1152]{1,0:T(8,128)(2,1)S(1)} %get-tuple-element.13.refs_1_, f32[1,256]{1,0:T(1,128)S(1)} %get-tuple-element.14.refs_2_, ...), custom_call_target="tpu_custom_call" | custom-call | tf_op jit(solution)/shard_map/write_out/pallas_call | solution.py:396

commit v4 on v3

--- a/solution.py
+++ b/solution.py
@@ -21,6 +21,8 @@
 KEEP = 96
 WIN = 384
 RING = 8
+QKV_CUTS = ((0, 512), (512, 3 * BW))
+DOWN_CUTS = ((0, 512), (512, 1024), (1024, D))
 F32 = jnp.float32
 BF16 = jnp.bfloat16
 
@@ -30,6 +32,10 @@
     centred = values - average
     spread = jnp.mean(centred * centred, axis=-1, keepdims=True)
     return centred * lax.rsqrt(spread + NORM_EPS)
+
+
+def dot(a, b):
+    return jnp.dot(a, b, preferred_element_type=F32)
 
 
 def dot_t(a, b):
@@ -73,6 +79,11 @@
     wd_v,
     fw_v,
     noisy_v,
+    wqt,
+    wot,
+    fwt,
+    sc,
+    pb,
     x1,
     qs,
     qr,
@@ -176,13 +187,28 @@
         kv[k * TOK : (k + 1) * TOK, :] = jnp.where(patch <= k, high, low)
 
     c_wq.wait()
+    for c in range(0, D, 128):
+        wqt[c : c + 128, :] = wq_v[:, c : c + 128].T
     c_q = []
     for o in halves:
         arrive_all(c_x[o])
-        qkv = dot_t(x1[o].reshape(GROUPS * HALF, D), wq_v[...]).astype(BF16)
-        qs[o] = qkv.reshape(GROUPS, HALF, 3 * BW)
-        c_q.append([remote(qs.at[o, slot], qr.at[o, mine], dev) for slot, dev, _ in homeward])
-        qr[o, mine] = qkv[0:HALF]
+        c_q.append([])
+        for a, b in QKV_CUTS:
+            qkv = dot(x1[o].reshape(GROUPS * HALF, D), wqt[:, a:b]).astype(BF16)
+            qs[o, :, :, a:b] = qkv.reshape(GROUPS, HALF, b - a)
+            c_q[o] += [
+                remote(qs.at[o, slot, :, a:b], qr.at[o, mine, :, a:b], dev)
+                for slot, dev, _ in homeward
+            ]
+            qr[o, mine, :, a:b] = qkv[0:HALF]
+
+    c_wo.wait()
+    for c in range(0, D, 128):
+        wot[c : c + 128, :] = wo_v[:, c : c + 128].T
+    c_fw.wait()
+    channels = fw_v.shape[0]
+    spots = HALF * channels
+    fwt[...] = jnp.concatenate([fw_v[...]] * HALF, axis=0).T
 
     queries = []
     for o in halves:
@@ -195,25 +221,30 @@
         kv[pl.ds(KEEP + rows[o], HALF), :] = fresh.astype(BF16)
 
     lane = lax.broadcasted_iota(jnp.int32, (HALF, WIN), 1)
-    c_wo.wait()
+
+    def heads_of(j):
+        starts = [TOK * j + a * HEAD for a in range(HEADS // GROUPS)]
+        return [(lane >= low) & (lane < low + HEAD) for low in starts]
+
+    block = (HEADS // GROUPS) * HALF
     c_m = []
     for o in halves:
+        for j in range(GROUPS):
+            q = queries[o][:, 256 * j : 256 * j + WIN]
+            spread = jnp.concatenate([jnp.where(m, q, 0.0) for m in heads_of(j)], axis=0)
+            sc[j * block : (j + 1) * block, :] = dot_t(
+                spread.astype(BF16), kv[:, 256 * j : 256 * j + WIN]
+            ) * HEAD ** (-0.5)
+        scores = sc[...]
+        raised = jnp.exp(scores - jnp.max(scores, axis=-1, keepdims=True))
+        pb[...] = (raised / jnp.sum(raised, axis=-1, keepdims=True)).astype(BF16)
         wins = []
         for j in range(GROUPS):
-            q = queries[o][:, 256 * j : 256 * j + WIN]
-            masks = [
-                (lane >= TOK * j + a * HEAD) & (lane < TOK * j + (a + 1) * HEAD)
-                for a in range(HEADS // GROUPS)
-            ]
-            spread = jnp.concatenate([jnp.where(m, q, 0.0) for m in masks], axis=0).astype(BF16)
-            scores = dot_t(spread, kv[:, 256 * j : 256 * j + WIN]) * HEAD ** (-0.5)
-            raised = jnp.exp(scores - jnp.max(scores, axis=-1, keepdims=True))
-            probs = (raised / jnp.sum(raised, axis=-1, keepdims=True)).astype(BF16)
-            mixed = jnp.dot(
-                probs, kv[:, D + 256 * j : D + 256 * j + WIN], preferred_element_type=F32
+            mixed = dot(
+                pb[j * block : (j + 1) * block, :], kv[:, D + 256 * j : D + 256 * j + WIN]
             )
             picked = jnp.zeros((HALF, WIN), F32)
-            for a, m in enumerate(masks):
+            for a, m in enumerate(heads_of(j)):
                 picked = jnp.where(m, mixed[a * HALF : (a + 1) * HALF], picked)
             wins.append(picked)
         cuts = [wins[0][:, 0:256]]
@@ -227,7 +258,7 @@
     c_p = []
     for o in halves:
         arrive_all(c_m[o])
-        proj = dot_t(x2[o].reshape(GROUPS * HALF, D), wo_v[...]).astype(BF16)
+        proj = dot(x2[o].reshape(GROUPS * HALF, D), wot[...]).astype(BF16)
         ps[o] = proj.reshape(GROUPS, HALF, BW)
         c_p.append([remote(ps.at[o, slot], pr.at[o, mine], dev) for slot, dev, _ in homeward])
         pr[o, mine] = proj[0:HALF]
@@ -244,11 +275,6 @@
         c_u.append(spread_tokens(x3, o))
 
     fresh_out[...] = kv[KEEP:, :]
-    c_fw.wait()
-    channels = fw_v.shape[0]
-    spots = HALF * channels
-    fw_tiled = jnp.concatenate([fw_v[...]] * HALF, axis=0)
-
     c_wu.wait()
     c_wd.wait()
     c_d = []
@@ -256,20 +282,39 @@
     for o in halves:
         arrive_all(c_u[o])
         inner_v[...] = jax.nn.gelu(
-            jnp.dot(x3[o].reshape(GROUPS * HALF, D), wu_v[...], preferred_element_type=F32),
-            approximate=True,
+            dot(x3[o].reshape(GROUPS * HALF, D), wu_v[...]), approximate=True
         ).astype(BF16)
-        part = jnp.dot(inner_v[...], wd_v[...], preferred_element_type=F32)
-        own.append(part[0:HALF])
-        parts[o] = part.astype(BF16).reshape(GROUPS, HALF, D)
-        c_d.append(
-            [remote(parts.at[o, slot], r4.at[o, i - 1], dev) for slot, dev, i in homeward]
-        )
+        own.append([])
+        c_d.append([])
+        for a, b in DOWN_CUTS:
+            part = dot(inner_v[...], wd_v[:, a:b])
+            own[o].append(part[0:HALF])
+            parts[o, :, :, a:b] = part.astype(BF16).reshape(GROUPS, HALF, b - a)
+            c_d[o] += [
+                remote(parts.at[o, slot, :, a:b], r4.at[o, i - 1, :, a:b], dev)
+                for slot, dev, i in homeward
+            ]
+
+    c_tm.wait()
+    c_gp.wait()
+    now = jnp.full((1, spots), time_ref[0], jnp.int32)
+    before = jnp.full((1, spots), time_ref[0] - gap_ref[0], jnp.int32)
+    now_bar = alpha_bar(now.astype(F32))
+    prev_bar = alpha_bar(before.astype(F32))
+    now_noise = jnp.sqrt(1.0 - now_bar)
+    now_root = jnp.sqrt(now_bar)
+    prev_noise = jnp.sqrt(1.0 - prev_bar)
+    prev_root = jnp.sqrt(prev_bar)
+    row = lax.broadcasted_iota(jnp.int32, (HALF, spots), 0)
+    col = lax.broadcasted_iota(jnp.int32, (HALF, spots), 1)
+    token = lax.div(col, channels) == row
+    c_fm.wait()
+    c_nz.wait()
 
     outs = []
     for o in halves:
         arrive_all(c_d[o])
-        total = own[o]
+        total = jnp.concatenate(own[o], axis=1)
         for i in range(GROUPS - 1):
             total = total + r4[o, i].astype(F32)
         outs.append((kept[o] + mod_v[5] * total).astype(BF16))
@@ -277,26 +322,16 @@
             leave[...] = outs[0]
             c_a = remote(leave, arrive, other)
 
-    c_fm.wait()
-    c_nz.wait()
-    c_tm.wait()
-    c_gp.wait()
     c_a.wait_recv()
     arrived = arrive[...]
     next_out[...] = jnp.where(flip, outs[1], arrived)
     final_rows = jnp.where(flip, arrived, outs[1]).astype(F32)
     shifted = (layer_norm(final_rows) * (1.0 + fmod_v[1:2, :]) + fmod_v[0:1, :]).astype(BF16)
-    each = dot_t(shifted, fw_tiled)
-    row = lax.broadcasted_iota(jnp.int32, (HALF, spots), 0)
-    col = lax.broadcasted_iota(jnp.int32, (HALF, spots), 1)
-    noise = jnp.sum(jnp.where(lax.div(col, channels) == row, each, 0.0), axis=0, keepdims=True)
-    now = jnp.full((1, spots), time_ref[0], jnp.int32)
-    before = jnp.full((1, spots), time_ref[0] - gap_ref[0], jnp.int32)
-    now_bar = alpha_bar(now.astype(F32))
-    prev_bar = alpha_bar(before.astype(F32))
-    clean = (noisy_v[...] - jnp.sqrt(1.0 - now_bar) * noise) / jnp.sqrt(now_bar)
+    each = dot(shifted, fwt[...])
+    noise = jnp.sum(jnp.where(token, each, 0.0), axis=0, keepdims=True)
+    clean = (noisy_v[...] - now_noise * noise) / now_root
     noise_out[...] = noise
-    den_out[...] = jnp.sqrt(prev_bar) * clean + jnp.sqrt(1.0 - prev_bar) * noise
+    den_out[...] = prev_root * clean + prev_noise * noise
 
     for c in sends:
         c.wait_send()
@@ -332,7 +367,7 @@
     any_spec = pl.BlockSpec(memory_space=pltpu.HBM)
     vmem = pl.BlockSpec(memory_space=pltpu.VMEM)
     spots = noisy_latent.shape[1]
-    remote_count = 37
+    remote_count = 55
     outs = pl.pallas_call(
         kernel,
         name="relay_step",
@@ -358,6 +393,11 @@
             pltpu.VMEM((D, D), BF16),
             pltpu.VMEM(final_weight.shape[::-1], BF16),
             pltpu.VMEM((1, spots), F32),
+            pltpu.VMEM((D, 3 * BW), BF16),
+            pltpu.VMEM((D, BW), BF16),
+            pltpu.VMEM((D, spots), BF16),
+            pltpu.VMEM((HEADS * HALF, KEEP + TOK), F32),
+            pltpu.VMEM((HEADS * HALF, KEEP + TOK), BF16),
             pltpu.VMEM((2, GROUPS, HALF, D), BF16),
             pltpu.VMEM((2, GROUPS, HALF, 3 * BW), BF16),
             pltpu.VMEM((2, GROUPS, HALF, 3 * BW), BF16),

time: 42.8 us -> 41.8 us (0.977)
  Pallas kernels: 40.1 us -> 39.1 us
    pallas_call x1, Pallas kernels: 39.4 us -> 38.4 us  [per_device(): pl.pallas_call(kernel, name='relay_step', out_shape=(jax.ShapeDtypeStruct...]
where the time goes in v4:
time: 41.8 us; the launch traced here: 41.7 us
  Pallas kernels  39.1 us (94%)
  between operations  2.58 us (6%)
    pallas_call x1, Pallas kernels, per_device(): pl.pallas_call(kernel, name='relay_step', out_shape=(jax.ShapeDtypeStruct...  38.4 us

profile of v4, /device:TPU:1, one launch (start us, length us, event | category | flops | bytes accessed | tf_op | source)
XLA Modules:
  0.0 41.7 jit_solution(12991557368993863670)
XLA Ops:
  2.6 38.4 %relay_step.1 = (bf16[32,2304]{1,0:T(8,128)(2,1)S(1)}, bf16[16,1152]{1,0:T(8,128)(2,1)S(1)}, f32[1,256]{1,0:T(1,128)S(1)}, f32[1,256]{1,0:T(1,128)S(1)}) custom-call(s32[1,1]{1,0:T(1,128)S(6)} %copy.17.patch_hbm, s32[1]{0:T(128)S(6)} %copy.18.time_hbm, s32[1]{0:T(128)S(6)} %copy.19.gap_hbm, bf16[32,1152]{1,0:T(8,128)(2,1)} %bitcast.20, ...), custom_call_target="tpu_custom_call" | custom-call | tf_op jit(solution)/shard_map/relay_step/pallas_call | solution.py:371
  41.0 0.7 %write_out.1 = (bf16[32,2304]{1,0:T(8,128)(2,1)}, bf16[16,1152]{1,0:T(8,128)(2,1)}, f32[1,256]{1,0:T(1,128)}, f32[1,256]{1,0:T(1,128)}) custom-call(bf16[32,2304]{1,0:T(8,128)(2,1)S(1)} %get-tuple-element.12.refs_0_, bf16[16,1152]{1,0:T(8,128)(2,1)S(1)} %get-tuple-element.13.refs_1_, f32[1,256]{1,0:T(1,128)S(1)} %get-tuple-element.14.refs_2_, ...), custom_call_target="tpu_custom_call" | custom-call | tf_op jit(solution)/shard_map/write_out/pallas_call | solution.py:436

commit v5 on v4

--- a/solution.py
+++ b/solution.py
@@ -95,8 +95,10 @@
     inner_v,
     parts,
     r4,
+    rx,
     leave,
     arrive,
+    gate,
     lsem,
     ssem,
     rsem,
@@ -108,13 +110,18 @@
     odd = lax.rem(z, 2)
     mine = lax.rem(z, GROUPS)
 
-    def at(dz):
-        return (s, base + lax.rem(z + dz + RING, RING))
-
-    far = 2 - 4 * odd
-    outward = [(at(far), 3), (at(1), 2), (at(-1), 1)]
-    homeward = [(3, at(-far), 3), (1, at(1), 2), (2, at(-1), 1)]
-    other = (1 - s, r)
+    def at(dz, section=s):
+        return (section, base + lax.rem(z + dz + RING, RING))
+
+    swap = 2 - 4 * lax.rem(lax.div(z, 2), 2)
+    skip = 2 - 4 * odd
+    far_to = (swap, skip)
+    far_from = (swap, -skip)
+    outward = [[(at(far), 3), (at(1), 2), (at(-1), 1)] for far in far_to]
+    homeward = [[(3, at(far), 3), (1, at(1), 2), (2, at(-1), 1)] for far in far_from]
+    across = 1 - s
+    other = (across, r)
+    crossing = [(3, at(far_from[0], across), 3), (1, at(1, across), 2), (2, at(-1, across), 1)]
     rows = [pl.multiple_of(HALF * (1 - s), HALF), pl.multiple_of(HALF * s, HALF)]
     halves = (0, 1)
 
@@ -126,11 +133,13 @@
         local.append(copy)
         return copy
 
+    barrier = pltpu.get_barrier_semaphore()
+    steps = (2, -2, 1, -1)
+    peers = [at(dz) for dz in steps] + [at(dz, across) for dz in steps] + [other]
+    for peer in peers:
+        pl.semaphore_signal(barrier, inc=1, device_id=peer, device_id_type=MESH)
     c_h = load(0, h_hbm, h_v)
     c_mod = load(1, mod_hbm, mod_v)
-    barrier = pltpu.get_barrier_semaphore()
-    for peer in (at(1), at(-1), at(2), at(-2), other):
-        pl.semaphore_signal(barrier, inc=1, device_id=peer, device_id_type=MESH)
     c_wq = load(3, wq_hbm, wq_v)
     c_pt = load(10, patch_hbm, patch_ref)
     c_st = load(2, stale_hbm, st_v)
@@ -162,7 +171,7 @@
         return copy
 
     def spread_tokens(buf, o):
-        return [remote(buf.at[o, 0], buf.at[o, slot], dev) for dev, slot in outward]
+        return [remote(buf.at[o, 0], buf.at[o, slot], dev) for dev, slot in outward[o]]
 
     def arrive_all(copies):
         for c in copies:
@@ -175,7 +184,7 @@
     x1[0, 0] = jnp.where(flip, normed[HALF:], normed[:HALF]).astype(BF16)
     x1[1, 0] = jnp.where(flip, normed[:HALF], normed[HALF:]).astype(BF16)
 
-    pl.semaphore_wait(barrier, 5)
+    pl.semaphore_wait(barrier, len(peers))
     c_x = [spread_tokens(x1, o) for o in halves]
 
     c_st.wait()
@@ -198,7 +207,7 @@
             qs[o, :, :, a:b] = qkv.reshape(GROUPS, HALF, b - a)
             c_q[o] += [
                 remote(qs.at[o, slot, :, a:b], qr.at[o, mine, :, a:b], dev)
-                for slot, dev, _ in homeward
+                for slot, dev, _ in homeward[o]
             ]
             qr[o, mine, :, a:b] = qkv[0:HALF]
 
@@ -220,39 +229,39 @@
         )
         kv[pl.ds(KEEP + rows[o], HALF), :] = fresh.astype(BF16)
 
-    lane = lax.broadcasted_iota(jnp.int32, (HALF, WIN), 1)
+    lane = lax.broadcasted_iota(jnp.int32, (TOK, WIN), 1)
 
     def heads_of(j):
         starts = [TOK * j + a * HEAD for a in range(HEADS // GROUPS)]
         return [(lane >= low) & (lane < low + HEAD) for low in starts]
 
-    block = (HEADS // GROUPS) * HALF
+    block = (HEADS // GROUPS) * TOK
+    query = jnp.concatenate(queries, axis=0)
+    for j in range(GROUPS):
+        q = query[:, 256 * j : 256 * j + WIN]
+        spread = jnp.concatenate([jnp.where(m, q, 0.0) for m in heads_of(j)], axis=0)
+        sc[j * block : (j + 1) * block, :] = dot_t(
+            spread.astype(BF16), kv[:, 256 * j : 256 * j + WIN]
+        ) * HEAD ** (-0.5)
+    scores = sc[...]
+    raised = jnp.exp(scores - jnp.max(scores, axis=-1, keepdims=True))
+    pb[...] = (raised / jnp.sum(raised, axis=-1, keepdims=True)).astype(BF16)
+    wins = []
+    for j in range(GROUPS):
+        mixed = dot(pb[j * block : (j + 1) * block, :], kv[:, D + 256 * j : D + 256 * j + WIN])
+        picked = jnp.zeros((TOK, WIN), F32)
+        for a, m in enumerate(heads_of(j)):
+            picked = jnp.where(m, mixed[a * TOK : (a + 1) * TOK], picked)
+        wins.append(picked)
+    cuts = [wins[0][:, 0:256]]
+    for j in range(1, GROUPS):
+        cuts.append(wins[j - 1][:, 256:WIN] + wins[j][:, 0:128])
+        cuts.append(wins[j][:, 128:256])
+    cuts.append(wins[GROUPS - 1][:, 256:WIN])
+    whole = jnp.concatenate(cuts, axis=1).astype(BF16)
     c_m = []
     for o in halves:
-        for j in range(GROUPS):
-            q = queries[o][:, 256 * j : 256 * j + WIN]
-            spread = jnp.concatenate([jnp.where(m, q, 0.0) for m in heads_of(j)], axis=0)
-            sc[j * block : (j + 1) * block, :] = dot_t(
-                spread.astype(BF16), kv[:, 256 * j : 256 * j + WIN]
-            ) * HEAD ** (-0.5)
-        scores = sc[...]
-        raised = jnp.exp(scores - jnp.max(scores, axis=-1, keepdims=True))
-        pb[...] = (raised / jnp.sum(raised, axis=-1, keepdims=True)).astype(BF16)
-        wins = []
-        for j in range(GROUPS):
-            mixed = dot(
-                pb[j * block : (j + 1) * block, :], kv[:, D + 256 * j : D + 256 * j + WIN]
-            )
-            picked = jnp.zeros((HALF, WIN), F32)
-            for a, m in enumerate(heads_of(j)):
-                picked = jnp.where(m, mixed[a * HALF : (a + 1) * HALF], picked)
-            wins.append(picked)
-        cuts = [wins[0][:, 0:256]]
-        for j in range(1, GROUPS):
-            cuts.append(wins[j - 1][:, 256:WIN] + wins[j][:, 0:128])
-            cuts.append(wins[j][:, 128:256])
-        cuts.append(wins[GROUPS - 1][:, 256:WIN])
-        x2[o, 0] = jnp.concatenate(cuts, axis=1).astype(BF16)
+        x2[o, 0] = whole[o * HALF : (o + 1) * HALF]
         c_m.append(spread_tokens(x2, o))
 
     c_p = []
@@ -260,7 +269,7 @@
         arrive_all(c_m[o])
         proj = dot(x2[o].reshape(GROUPS * HALF, D), wot[...]).astype(BF16)
         ps[o] = proj.reshape(GROUPS, HALF, BW)
-        c_p.append([remote(ps.at[o, slot], pr.at[o, mine], dev) for slot, dev, _ in homeward])
+        c_p.append([remote(ps.at[o, slot], pr.at[o, mine], dev) for slot, dev, _ in homeward[o]])
         pr[o, mine] = proj[0:HALF]
 
     c_u = []
@@ -273,26 +282,31 @@
         middle = layer_norm(h1) * (1.0 + mod_v[4]) + mod_v[3]
         x3[o, 0] = middle.astype(BF16)
         c_u.append(spread_tokens(x3, o))
+        if o == 0:
+            leave[...] = h1
+            c_l = [remote(leave, arrive, other), remote(mod_v.at[5], gate, other)]
 
     fresh_out[...] = kv[KEEP:, :]
     c_wu.wait()
     c_wd.wait()
+    early = list(sends)
     c_d = []
-    own = []
     for o in halves:
         arrive_all(c_u[o])
         inner_v[...] = jax.nn.gelu(
             dot(x3[o].reshape(GROUPS * HALF, D), wu_v[...]), approximate=True
         ).astype(BF16)
-        own.append([])
+        own = []
         c_d.append([])
         for a, b in DOWN_CUTS:
             part = dot(inner_v[...], wd_v[:, a:b])
-            own[o].append(part[0:HALF])
+            own.append(part[0:HALF])
             parts[o, :, :, a:b] = part.astype(BF16).reshape(GROUPS, HALF, b - a)
+            routes = crossing + [(0, other, GROUPS)] if o == 0 else homeward[o]
+            into = rx if o == 0 else r4
             c_d[o] += [
-                remote(parts.at[o, slot, :, a:b], r4.at[o, i - 1, :, a:b], dev)
-                for slot, dev, i in homeward
+                remote(parts.at[o, slot, :, a:b], into.at[i - 1, :, a:b], dev)
+                for slot, dev, i in routes
             ]
 
     c_tm.wait()
@@ -310,22 +324,25 @@
     token = lax.div(col, channels) == row
     c_fm.wait()
     c_nz.wait()
-
-    outs = []
-    for o in halves:
-        arrive_all(c_d[o])
-        total = jnp.concatenate(own[o], axis=1)
-        for i in range(GROUPS - 1):
-            total = total + r4[o, i].astype(F32)
-        outs.append((kept[o] + mod_v[5] * total).astype(BF16))
-        if o == 0:
-            leave[...] = outs[0]
-            c_a = remote(leave, arrive, other)
-
-    c_a.wait_recv()
-    arrived = arrive[...]
-    next_out[...] = jnp.where(flip, outs[1], arrived)
-    final_rows = jnp.where(flip, arrived, outs[1]).astype(F32)
+    for c in early:
+        c.wait_send()
+
+    arrive_all(c_l)
+    arrive_all(c_d[0])
+    total = rx[0].astype(F32)
+    for i in range(1, GROUPS):
+        total = total + rx[i].astype(F32)
+    out_across = arrive[...] + gate[...] * total
+    for c in c_d[0]:
+        c.wait_send()
+
+    arrive_all(c_d[1])
+    total = jnp.concatenate(own, axis=1)
+    for i in range(GROUPS - 1):
+        total = total + r4[i].astype(F32)
+    out_here = kept[1] + mod_v[5] * total
+    next_out[...] = jnp.where(flip, out_here, out_across).astype(BF16)
+    final_rows = jnp.where(flip, out_across, out_here).astype(BF16).astype(F32)
     shifted = (layer_norm(final_rows) * (1.0 + fmod_v[1:2, :]) + fmod_v[0:1, :]).astype(BF16)
     each = dot(shifted, fwt[...])
     noise = jnp.sum(jnp.where(token, each, 0.0), axis=0, keepdims=True)
@@ -333,7 +350,7 @@
     noise_out[...] = noise
     den_out[...] = prev_root * clean + prev_noise * noise
 
-    for c in sends:
+    for c in c_d[1]:
         c.wait_send()
 
 
@@ -367,7 +384,7 @@
     any_spec = pl.BlockSpec(memory_space=pltpu.HBM)
     vmem = pl.BlockSpec(memory_space=pltpu.VMEM)
     spots = noisy_latent.shape[1]
-    remote_count = 55
+    remote_count = 59
     outs = pl.pallas_call(
         kernel,
         name="relay_step",
@@ -396,8 +413,8 @@
             pltpu.VMEM((D, 3 * BW), BF16),
             pltpu.VMEM((D, BW), BF16),
             pltpu.VMEM((D, spots), BF16),
-            pltpu.VMEM((HEADS * HALF, KEEP + TOK), F32),
-            pltpu.VMEM((HEADS * HALF, KEEP + TOK), BF16),
+            pltpu.VMEM((HEADS * TOK, KEEP + TOK), F32),
+            pltpu.VMEM((HEADS * TOK, KEEP + TOK), BF16),
             pltpu.VMEM((2, GROUPS, HALF, D), BF16),
             pltpu.VMEM((2, GROUPS, HALF, 3 * BW), BF16),
             pltpu.VMEM((2, GROUPS, HALF, 3 * BW), BF16),
@@ -408,9 +425,11 @@
             pltpu.VMEM((2, GROUPS, HALF, D), BF16),
             pltpu.VMEM((GROUPS * HALF, D), BF16),
             pltpu.VMEM((2, GROUPS, HALF, D), BF16),
-            pltpu.VMEM((2, GROUPS - 1, HALF, D), BF16),
-            pltpu.VMEM((HALF, D), BF16),
-            pltpu.VMEM((HALF, D), BF16),
+            pltpu.VMEM((GROUPS - 1, HALF, D), BF16),
+            pltpu.VMEM((GROUPS, HALF, D), BF16),
+            pltpu.VMEM((HALF, D), F32),
+            pltpu.VMEM((HALF, D), F32),
+            pltpu.VMEM((1, D), F32),
             pltpu.SemaphoreType.DMA((13,)),
             pltpu.SemaphoreType.DMA((remote_count,)),
             pltpu.SemaphoreType.DMA((remote_count,)),

time: 41.8 us -> 41.1 us (0.983); the launches traced: 41.7 us -> 40.5 us
  Pallas kernels: 39.1 us -> 37.9 us
    pallas_call x1, Pallas kernels: 38.4 us -> 37.2 us  [per_device(): pl.pallas_call(kernel, name='relay_step', out_shape=(jax.ShapeDtypeStruct...]
where the time goes in v5:
time: 41.1 us; the launch traced here: 40.5 us
  Pallas kernels  37.9 us (92%)
  between operations  2.58 us (6%)
    pallas_call x1, Pallas kernels, per_device(): pl.pallas_call(kernel, name='relay_step', out_shape=(jax.ShapeDtypeStruct...  37.2 us

profile of v5, /device:TPU:1, one launch (start us, length us, event | category | flops | bytes accessed | tf_op | source)
XLA Modules:
  0.0 40.5 jit_solution(3077447114953716808)
XLA Ops:
  2.6 37.2 %relay_step.1 = (bf16[32,2304]{1,0:T(8,128)(2,1)S(1)}, bf16[16,1152]{1,0:T(8,128)(2,1)S(1)}, f32[1,256]{1,0:T(1,128)S(1)}, f32[1,256]{1,0:T(1,128)S(1)}) custom-call(s32[1,1]{1,0:T(1,128)S(6)} %copy.17.patch_hbm, s32[1]{0:T(128)S(6)} %copy.18.time_hbm, s32[1]{0:T(128)S(6)} %copy.19.gap_hbm, bf16[32,1152]{1,0:T(8,128)(2,1)} %bitcast.20, ...), custom_call_target="tpu_custom_call" | custom-call | tf_op jit(solution)/shard_map/relay_step/pallas_call | solution.py:388
  39.8 0.7 %write_out.1 = (bf16[32,2304]{1,0:T(8,128)(2,1)}, bf16[16,1152]{1,0:T(8,128)(2,1)}, f32[1,256]{1,0:T(1,128)}, f32[1,256]{1,0:T(1,128)}) custom-call(bf16[32,2304]{1,0:T(8,128)(2,1)S(1)} %get-tuple-element.12.refs_0_, bf16[16,1152]{1,0:T(8,128)(2,1)S(1)} %get-tuple-element.13.refs_1_, f32[1,256]{1,0:T(1,128)S(1)} %get-tuple-element.14.refs_2_, ...), custom_call_target="tpu_custom_call" | custom-call | tf_op jit(solution)/shard_map/write_out/pallas_call | solution.py:455

commit v6 on v5

--- a/solution.py
+++ b/solution.py
@@ -21,8 +21,8 @@
 KEEP = 96
 WIN = 384
 RING = 8
-QKV_CUTS = ((0, 512), (512, 3 * BW))
-DOWN_CUTS = ((0, 512), (512, 1024), (1024, D))
+QKV_CUTS = ((0, 3 * BW),)
+DOWN_CUTS = ((0, 768), (768, D))
 F32 = jnp.float32
 BF16 = jnp.bfloat16
 
@@ -384,7 +384,7 @@
     any_spec = pl.BlockSpec(memory_space=pltpu.HBM)
     vmem = pl.BlockSpec(memory_space=pltpu.VMEM)
     spots = noisy_latent.shape[1]
-    remote_count = 59
+    remote_count = 46
     outs = pl.pallas_call(
         kernel,
         name="relay_step",

time: 41.1 us -> 40.7 us (level)
  the two profiles are of different devices: /device:TPU:1 before, /device:TPU:10 now
where the time goes in v6:
time: 40.7 us; the launch traced here: 40.6 us
  Pallas kernels  38 us (93%)
  between operations  2.58 us (6%)
    pallas_call x1, Pallas kernels, per_device(): pl.pallas_call(kernel, name='relay_step', out_shape=(jax.ShapeDtypeStruct...  37.3 us

profile of v6, /device:TPU:10, one launch (start us, length us, event | category | flops | bytes accessed | tf_op | source)
XLA Modules:
  0.0 40.6 jit_solution(1231058225755933723)
XLA Ops:
  2.6 37.3 %relay_step.1 = (bf16[32,2304]{1,0:T(8,128)(2,1)S(1)}, bf16[16,1152]{1,0:T(8,128)(2,1)S(1)}, f32[1,256]{1,0:T(1,128)S(1)}, f32[1,256]{1,0:T(1,128)S(1)}) custom-call(s32[1,1]{1,0:T(1,128)S(6)} %copy.17.patch_hbm, s32[1]{0:T(128)S(6)} %copy.18.time_hbm, s32[1]{0:T(128)S(6)} %copy.19.gap_hbm, bf16[32,1152]{1,0:T(8,128)(2,1)} %bitcast.20, ...), custom_call_target="tpu_custom_call" | custom-call | tf_op jit(solution)/shard_map/relay_step/pallas_call | solution.py:388
  39.8 0.7 %write_out.1 = (bf16[32,2304]{1,0:T(8,128)(2,1)}, bf16[16,1152]{1,0:T(8,128)(2,1)}, f32[1,256]{1,0:T(1,128)}, f32[1,256]{1,0:T(1,128)}) custom-call(bf16[32,2304]{1,0:T(8,128)(2,1)S(1)} %get-tuple-element.12.refs_0_, bf16[16,1152]{1,0:T(8,128)(2,1)S(1)} %get-tuple-element.13.refs_1_, f32[1,256]{1,0:T(1,128)S(1)} %get-tuple-element.14.refs_2_, ...), custom_call_target="tpu_custom_call" | custom-call | tf_op jit(solution)/shard_map/write_out/pallas_call | solution.py:455
